TPU v7x, 32 devices: a whole 2x2x4 slice. The times are simulated.
32 devices in a mesh: seq: 8 (over z, x), exp: 4 (over y, core).
Axes of the slice: x: 2, y: 2, z: 4, core: 2. Of those that a mesh axis runs over, the one named last changes fastest.
Arguments:
- queries: bfloat16 [1024, 4096], P('seq', 'exp'), may hold values from -2 to 2
- keys: bfloat16 [1024, 4096], P('seq', 'exp'), may hold values from -2 to 2
- values: bfloat16 [1024, 4096], P('seq', 'exp'), may hold values from -6 to 6
- log_decay: float32 [1024, 32], P('seq', 'exp'), may hold values from -1 to 0, as said below
- residual: bfloat16 [1024, 4096], P(('seq', 'exp')), may hold values from -6 to 6
- attn_gain: float32 [4096], replicated, may hold values from 0.25 to 1.75
- moe_gain: float32 [4096], replicated, may hold values from 0.25 to 1.75
- expert_ids: int32 [1024, 2], P(('seq', 'exp')), may hold values from 0 to 3, all different within a row; in each aligned block of 32 rows (0 to 31, 32 to 63, ...) at most 24 rows name the same one
- gate_weights: float32 [1024, 2], P(('seq', 'exp')), may hold values from 0.2 to 1
- w_gate: bfloat16 [4, 9216, 4096], P('exp', 'seq'), may hold values from -0.09375 to 0.09375
- w_up: bfloat16 [4, 9216, 4096], P('exp', 'seq'), may hold values from -0.09375 to 0.09375
- w_down: bfloat16 [4, 9216, 4096], P('exp', 'seq'), may hold values from -0.0625 to 0.0625
Outputs:
- layer_out: bfloat16 [1024, 4096], P(('seq', 'exp'))
Inputs may be any that keep to these rules, and one draw needn't show every extreme that they name: `expert_ids`: each token names two different experts. In each aligned block of 32 tokens (the tokens of one device) no expert is named by more than 24 tokens, a bound that some block reaches. `log_decay`: every entry is negative.
All inputs are finite; a program needn't handle non-finite values.
Results may differ from a plain program's by a relative error of at most 0.012.
Values may be sent and summed in bfloat16 or wider, within the bound.
A program may use at most 128 MiB of HBM per device.

v0:
```python
import functools

import jax
import jax.numpy as jnp
from jax import lax
from jax.experimental import pallas as pl
from jax.experimental.pallas import tpu as pltpu
from jax.sharding import PartitionSpec as P

MESH = pl.DeviceIdType.MESH
PARTS = 2


class Place:
    def __init__(self, n_seq, n_exp):
        s, e = lax.axis_index("seq"), lax.axis_index("exp")
        self.fold, self.n_exp = n_exp // 4, n_exp
        self.length = (n_seq // 2) * self.fold
        self.p = (s // 2) * self.fold + e // 4
        self.x, self.y, self.c = s % 2, (e // 2) % 2, e % 2

    def ids(self, p, x, y, c):
        return (p // self.fold) * 2 + x, (p % self.fold) * 4 + y * 2 + c

    def block(self, p, x, y, c):
        s, e = self.ids(p, x, y, c)
        return s * self.n_exp + e

    def dev(self, dp=0, dx=0, dy=0, dc=0):
        x = 1 - self.x if dx else self.x
        y = 1 - self.y if dy else self.y
        c = 1 - self.c if dc else self.c
        return self.ids(self.p + dp, x, y, c)

    def greet(self):
        barrier = pltpu.get_barrier_semaphore()
        for d in (dict(dx=1), dict(dy=1), dict(dc=1)):
            pl.semaphore_signal(barrier, inc=1, device_id=self.dev(**d), device_id_type=MESH)

        @pl.when(self.p > 0)
        def _():
            pl.semaphore_signal(barrier, inc=1, device_id=self.dev(dp=-1), device_id_type=MESH)

        @pl.when(self.p < self.length - 1)
        def _():
            pl.semaphore_signal(barrier, inc=1, device_id=self.dev(dp=1), device_id_type=MESH)

        ends = (self.p > 0).astype(jnp.int32) + (self.p < self.length - 1).astype(jnp.int32)
        pl.semaphore_wait(barrier, 3 + ends)

    def at(self, stage, sign, k):
        if sign == 0:
            stage(0, 0, 0)
        elif sign < 0:
            pl.when(self.p >= k)(lambda: stage(2 * k - 1, -k, -1))
        else:
            pl.when(self.p + k < self.length)(lambda: stage(2 * k, k, 1))

    def far_first(self, stage):
        def one(i, carry):
            for sign in (1, -1):
                self.at(stage, sign, self.length - 1 - i)
            return carry

        if self.length <= 8:
            for i in range(self.length - 1):
                one(i, 0)
        else:
            lax.fori_loop(0, self.length - 1, one, 0)
        self.at(stage, 0, 0)

    def near_first(self, *stages):
        depth = len(stages)

        def ring(stage, k):
            if isinstance(k, int) and k == 0:
                self.at(stage, 0, 0)
            else:
                for sign in (-1, 1):
                    self.at(stage, sign, k)

        def step(k):
            for j, stage in enumerate(stages):
                if 0 <= k - j < self.length:
                    ring(stage, k - j)

        total = self.length + depth - 1
        if self.length <= 8:
            for k in range(total):
                step(k)
            return
        for k in range(depth):
            step(k)

        def one(k, carry):
            for j, stage in enumerate(stages):
                ring(stage, k - j)
            return carry

        lax.fori_loop(depth, self.length, one, 0)
        for k in range(self.length, total):
            step(k)


def gather_kernel(n_seq, n_exp, x_ref, g_ref, out_ref, gout_ref, send, recv, loc):
    me = Place(n_seq, n_exp)
    rows, width = x_ref.shape
    grow = g_ref.shape[0]
    me.greet()

    def place(ref, off, dx, dy, dc=0):
        x = 1 - me.x if dx else me.x
        y = 1 - me.y if dy else me.y
        c = 1 - me.c if dc else me.c
        b = me.block(me.p + off, x, y, c)
        n = rows if ref is out_ref else grow
        return ref.at[pl.ds(pl.multiple_of(b * n, n), n)]

    def copies(part, kind, slot, off, dx, dy, to, own=False, half=None, dc=0):
        dst_x, dst_g = place(out_ref, off, dx, dy, dc), place(gout_ref, off, dx, dy, dc)
        src_x, src_g = (x_ref, g_ref) if own else (dst_x, dst_g)
        span = width // PARTS
        if half is None:
            cols = pl.ds(part * span, span)
        else:
            cols = pl.ds(part * span + half * (span // 2), span // 2)
        out = [
            pltpu.make_async_remote_copy(
                src_x.at[:, cols],
                dst_x.at[:, cols],
                send.at[kind, slot, part],
                recv.at[kind, slot, part],
                to,
                MESH,
            )
        ]
        if half != 1 and part == 0:
            out.append(
                pltpu.make_async_remote_copy(
                    src_g, dst_g, send.at[kind, slot, PARTS], recv.at[kind, slot, PARTS], to, MESH
                )
            )
        return out

    def start(*a, **k):
        for cp in copies(*a, **k):
            cp.start()

    def wait_recv(*a, **k):
        for cp in copies(*a, **k):
            cp.wait_recv()

    def wait_send(*a, **k):
        for cp in copies(*a, **k):
            cp.wait_send()

    left, right = dict(dp=-1), dict(dp=1)
    X, Y, C = me.dev(dx=1), me.dev(dy=1), me.dev(dc=1)

    def line_sends(off, sign, do):
        own = sign == 0
        if sign <= 0:
            pl.when(me.p + 1 < me.length)(
                lambda: do(0, 2 * (-off + 1) - 1, off, 0, 0, me.dev(**right), own=own)
            )
        if sign >= 0:
            pl.when(me.p > 0)(lambda: do(0, 2 * (off + 1), off, 0, 0, me.dev(**left), own=own))

    def stage_line(slot, off, sign, do):
        own = sign == 0
        line_sends(off, sign, do)
        do(1, slot, off, 0, 0, X, own=own)
        do(2, slot, off, 0, 0, Y, own=own)
        do(5, slot, off, 0, 0, C, own=own)

    def stage_xy_1(slot, off, do):
        do(3, slot, off, 1, 0, Y, half=0)
        do(6, slot, off, 1, 0, C)

    def stage_xy_2(slot, off, do):
        do(4, slot, off, 0, 1, X, half=1)
        do(7, slot, off, 0, 1, C)

    def stage_diag(slot, off, do):
        do(8, slot, off, 1, 1, C)

    local = [
        pltpu.make_async_copy(x_ref, place(out_ref, 0, 0, 0), loc.at[0]),
        pltpu.make_async_copy(g_ref, place(gout_ref, 0, 0, 0), loc.at[1]),
    ]
    for cp in local:
        cp.start()

    def s1(slot, off, sign):
        for part in range(PARTS):
            if sign:
                wait_recv(part, 0, slot, off, 0, 0, X)
            stage_line(slot, off, sign, functools.partial(start, part))

    def s2(slot, off, sign):
        for part in range(PARTS):
            wait_recv(part, 1, slot, off, 1, 0, X)
            stage_xy_1(slot, off, functools.partial(start, part))
            wait_recv(part, 2, slot, off, 0, 1, X)
            stage_xy_2(slot, off, functools.partial(start, part))

    def s3(slot, off, sign):
        for part in range(PARTS):
            wait_recv(part, 3, slot, off, 1, 1, X, half=0)
            wait_recv(part, 4, slot, off, 1, 1, X, half=1)
            stage_diag(slot, off, functools.partial(start, part))

    me.near_first(s1, s2, s3)

    def s4(slot, off, sign):
        for part in range(PARTS):
            done = functools.partial(wait_send, part)
            stage_line(slot, off, sign, done)
            stage_xy_1(slot, off, done)
            stage_xy_2(slot, off, done)
            stage_diag(slot, off, done)
            wait_recv(part, 5, slot, off, 0, 0, X, dc=1)
            wait_recv(part, 6, slot, off, 1, 0, X, dc=1)
            wait_recv(part, 7, slot, off, 0, 1, X, dc=1)
            wait_recv(part, 8, slot, off, 1, 1, X, dc=1)

    me.near_first(s4)
    for cp in local:
        cp.wait()


def gather_all(x, g, n_seq, n_exp):
    n = n_seq * n_exp
    length = n // 8
    anyspace = pl.BlockSpec(memory_space=pl.ANY)
    return pl.pallas_call(
        functools.partial(gather_kernel, n_seq, n_exp),
        out_shape=(
            jax.ShapeDtypeStruct((n * x.shape[0], x.shape[1]), x.dtype),
            jax.ShapeDtypeStruct((n * g.shape[0], g.shape[1]), g.dtype),
        ),
        in_specs=[anyspace, anyspace],
        out_specs=(anyspace, anyspace),
        scratch_shapes=[
            pltpu.SemaphoreType.DMA((9, 2 * length + 1, PARTS + 1)),
            pltpu.SemaphoreType.DMA((9, 2 * length + 1, PARTS + 1)),
            pltpu.SemaphoreType.DMA((2,)),
        ],
        compiler_params=pltpu.CompilerParams(collective_id=1, has_side_effects=True),
    )(x, g)


def scatter_kernel(
    n_seq, n_exp, y_ref, out_ref, acc, sib, xbuf, ybuf, dab, dbb, line, send, recv, loc
):
    me = Place(n_seq, n_exp)
    L = me.length
    rows, width = out_ref.shape
    halfw = width // 2
    me.greet()
    X, Y, C = me.dev(dx=1), me.dev(dy=1), me.dev(dc=1)

    def src(off, grp, dc):
        x = 1 - me.x if grp & 1 else me.x
        y = 1 - me.y if grp & 2 else me.y
        c = 1 - me.c if dc else me.c
        b = me.block(me.p + off, x, y, c)
        return y_ref.at[pl.ds(pl.multiple_of(b * rows, rows), rows)]

    def sib_copy(slot, off, grp):
        return pltpu.make_async_remote_copy(
            src(off, grp, 1), sib.at[grp, slot], send.at[grp, slot], recv.at[grp, slot], C, MESH
        )

    def load(slot, off, grp):
        return pltpu.make_async_copy(src(off, grp, 0), acc.at[grp, slot], loc.at[grp, slot])

    for grp in (3, 1, 2, 0):

        def go(slot, off, sign, grp=grp):
            sib_copy(slot, off, grp).start()
            load(slot, off, grp).start()

        me.far_first(go)

    f32 = jnp.float32

    def pair_sum(slot, off, grp):
        load(slot, off, grp).wait()
        sib_copy(slot, off, grp).wait_recv()
        return acc[grp, slot].astype(f32) + sib[grp, slot].astype(f32)

    def diag_a(slot):
        return pltpu.make_async_remote_copy(
            acc.at[3, slot, :, pl.ds(0, halfw)], dab.at[slot], send.at[4, slot], recv.at[4, slot], Y, MESH
        )

    def diag_b(slot):
        return pltpu.make_async_remote_copy(
            acc.at[3, slot, :, pl.ds(halfw, halfw)], dbb.at[slot], send.at[5, slot], recv.at[5, slot], X, MESH
        )

    def x_copy(slot):
        return pltpu.make_async_remote_copy(
            acc.at[1, slot], xbuf.at[slot], send.at[6, slot], recv.at[6, slot], X, MESH
        )

    def y_copy(slot):
        return pltpu.make_async_remote_copy(
            acc.at[2, slot], ybuf.at[slot], send.at[7, slot], recv.at[7, slot], Y, MESH
        )

    def line_copy(slot, sign):
        return pltpu.make_async_remote_copy(
            acc.at[0, slot],
            line.at[slot],
            send.at[8, slot],
            recv.at[8, slot],
            me.dev(dp=sign),
            MESH,
        )

    def d1(slot, off, sign):
        acc[3, slot] = pair_sum(slot, off, 3).astype(acc.dtype)
        diag_a(slot).start()
        diag_b(slot).start()

    def d2(slot, off, sign):
        sx = pair_sum(slot, off, 1)
        diag_a(slot).wait_recv()
        acc[1, slot, :, pl.ds(0, halfw)] = (sx[:, :halfw] + dab[slot].astype(f32)).astype(acc.dtype)
        acc[1, slot, :, pl.ds(halfw, halfw)] = sx[:, halfw:].astype(acc.dtype)
        x_copy(slot).start()
        sy = pair_sum(slot, off, 2)
        diag_b(slot).wait_recv()
        acc[2, slot, :, pl.ds(0, halfw)] = sy[:, :halfw].astype(acc.dtype)
        acc[2, slot, :, pl.ds(halfw, halfw)] = (sy[:, halfw:] + dbb[slot].astype(f32)).astype(acc.dtype)
        y_copy(slot).start()

    def d3(slot, off, sign):
        total = pair_sum(slot, off, 0)
        x_copy(slot).wait_recv()
        y_copy(slot).wait_recv()
        total = total + xbuf[slot].astype(f32) + ybuf[slot].astype(f32)
        if sign == 0:
            out_ref[...] = total
            if L > 1:

                @pl.when(me.p > 0)
                def _():
                    in_copy(2).wait_recv()
                    out_ref[...] += line[2].astype(f32)

                @pl.when(me.p < L - 1)
                def _():
                    in_copy(1).wait_recv()
                    out_ref[...] += line[1].astype(f32)

            return
        acc[0, slot] = total.astype(acc.dtype)
        far = slot + 2
        behind = me.p > 0 if sign > 0 else me.p < L - 1

        @pl.when(jnp.logical_and(behind, sign * off + 1 < L))
        def _():
            in_copy(far).wait_recv()
            acc[0, slot] = (acc[0, slot].astype(f32) + line[far].astype(f32)).astype(acc.dtype)

        line_copy(slot, sign).start()

    def in_copy(slot):
        return pltpu.make_async_remote_copy(
            acc.at[0, slot], line.at[slot], send.at[8, slot], recv.at[8, slot], X, MESH
        )

    me.far_first(d1)
    me.far_first(d2)
    me.far_first(d3)

    def fin(slot, off, sign):
        for grp in range(4):
            sib_copy(slot, off, grp).wait_send()
        diag_a(slot).wait_send()
        diag_b(slot).wait_send()
        x_copy(slot).wait_send()
        y_copy(slot).wait_send()
        if sign:
            line_copy(slot, sign).wait_send()

    me.far_first(fin)


def scatter_sum(part, n_seq, n_exp):
    n = n_seq * n_exp
    slots = n // 4 - 1 + 2
    rows, width = part.shape[0] // n, part.shape[1]
    bf = jnp.bfloat16
    return pl.pallas_call(
        functools.partial(scatter_kernel, n_seq, n_exp),
        out_shape=jax.ShapeDtypeStruct((rows, width), jnp.float32),
        in_specs=[pl.BlockSpec(memory_space=pl.ANY)],
        out_specs=pl.BlockSpec(memory_space=pltpu.VMEM),
        scratch_shapes=[
            pltpu.VMEM((4, slots, rows, width), bf),
            pltpu.VMEM((4, slots, rows, width), bf),
            pltpu.VMEM((slots, rows, width), bf),
            pltpu.VMEM((slots, rows, width), bf),
            pltpu.VMEM((slots, rows, width // 2), bf),
            pltpu.VMEM((slots, rows, width // 2), bf),
            pltpu.VMEM((slots, rows, width), bf),
            pltpu.SemaphoreType.DMA((9, slots)),
            pltpu.SemaphoreType.DMA((9, slots)),
            pltpu.SemaphoreType.DMA((4, slots)),
        ],
        compiler_params=pltpu.CompilerParams(
            collective_id=2, has_side_effects=True, vmem_limit_bytes=60 * 2**20
        ),
    )(part)


def carry_kernel(n_seq, own_ref, own16_ref, tot_ref, out_ref, peer, ptot, cin, cout, send, recv, tsem):
    s, e = lax.axis_index("seq"), lax.axis_index("exp")
    z, odd, deep = s // 2, s % 2, n_seq // 2
    heads = own_ref.shape[0]
    pair = (z * 2 + 1 - odd, e)

    barrier = pltpu.get_barrier_semaphore()
    pl.semaphore_signal(barrier, inc=1, device_id=pair, device_id_type=MESH)

    @pl.when(z > 0)
    def _():
        pl.semaphore_signal(barrier, inc=1, device_id=(s - 2, e), device_id_type=MESH)

    @pl.when(z < deep - 1)
    def _():
        pl.semaphore_signal(barrier, inc=1, device_id=(s + 2, e), device_id_type=MESH)

    ends = (z > 0).astype(jnp.int32) + (z < deep - 1).astype(jnp.int32)
    pl.semaphore_wait(barrier, 1 + ends)

    tot_copy = pltpu.make_async_remote_copy(tot_ref, ptot, tsem.at[0], tsem.at[1], pair, MESH)

    def pair_copy(h):
        return pltpu.make_async_remote_copy(
            own16_ref.at[h], peer.at[h], send.at[0, h], recv.at[0, h], pair, MESH
        )

    def line_copy(h):
        return pltpu.make_async_remote_copy(
            cout.at[h], cin.at[h], send.at[1, h], recv.at[1, h], (s + 2, e), MESH
        )

    tot_copy.start()
    for h in range(heads):
        pair_copy(h).start()

    @pl.when(z == 0)
    def _():
        cin[...] = jnp.zeros_like(cin)

    tot_copy.wait_recv()
    mine, other = tot_ref[...], ptot[...]
    both = jnp.exp(mine + other)
    is_odd = jnp.full(mine.shape, odd, jnp.int32) == 1
    one = jnp.ones_like(mine)
    own_by = jnp.where(is_odd, one, jnp.exp(other))
    peer_by = jnp.where(is_odd, jnp.exp(mine), one)
    carry_by = jnp.where(is_odd, jnp.exp(other), one)
    peer_in = jnp.where(is_odd, one, jnp.zeros_like(mine))
    for h in range(heads):
        pair_copy(h).wait_recv()

        @pl.when(z > 0)
        def _():
            line_copy(h).wait_recv()

        near = peer[h].astype(jnp.float32)
        come = cin[h].astype(jnp.float32)

        @pl.when(z < deep - 1)
        def _():
            cout[h] = (
                both[h : h + 1] * come + own_by[h : h + 1] * own_ref[h] + peer_by[h : h + 1] * near
            ).astype(cout.dtype)
            line_copy(h).start()

        out_ref[h] = carry_by[h : h + 1] * come + peer_in[h : h + 1] * near

    tot_copy.wait_send()
    for h in range(heads):
        pair_copy(h).wait_send()

        @pl.when(z < deep - 1)
        def _():
            line_copy(h).wait_send()


def carried_in(block_total, block_state, n_seq):
    heads, dim, _ = block_state.shape
    bf = jnp.bfloat16
    tile = jnp.pad(block_total, (0, -heads % 8))
    tile = jnp.broadcast_to(tile[:, None], (tile.shape[0], dim))
    vmem = pl.BlockSpec(memory_space=pltpu.VMEM)
    return pl.pallas_call(
        functools.partial(carry_kernel, n_seq),
        out_shape=jax.ShapeDtypeStruct(block_state.shape, jnp.float32),
        in_specs=[vmem] * 3,
        out_specs=vmem,
        scratch_shapes=[
            pltpu.VMEM(block_state.shape, bf),
            pltpu.VMEM(tile.shape, jnp.float32),
            pltpu.VMEM(block_state.shape, bf),
            pltpu.VMEM(block_state.shape, bf),
            pltpu.SemaphoreType.DMA((2, heads)),
            pltpu.SemaphoreType.DMA((2, heads)),
            pltpu.SemaphoreType.DMA((2,)),
        ],
        compiler_params=pltpu.CompilerParams(collective_id=3, has_side_effects=True),
    )(block_state, block_state.astype(bf), tile)


def mix_kernel(n_exp, normed_ref, res_ref, again_ref, mgain_ref, hid_ref, in_ref, tok, send, recv, loc):
    s, e = lax.axis_index("seq"), lax.axis_index("exp")
    rows, width = res_ref.shape[0], normed_ref.shape[1]

    barrier = pltpu.get_barrier_semaphore()
    for k in range(1, n_exp):
        pl.semaphore_signal(
            barrier, inc=1, device_id=(s, lax.rem(e + k, n_exp)), device_id_type=MESH
        )
    pl.semaphore_wait(barrier, n_exp - 1)

    def source(peer):
        return normed_ref.at[pl.ds(pl.multiple_of(peer * rows, rows), rows)]

    own = pltpu.make_async_copy(source(e), tok.at[e], loc.at[0])

    def copy(k):
        peer = lax.rem(e + k, n_exp)
        return pltpu.make_async_remote_copy(
            source(peer), tok.at[e], send.at[k], recv.at[k], (s, peer), MESH
        )

    def arriving(k):
        sender = lax.rem(e + n_exp - k, n_exp)
        return pltpu.make_async_remote_copy(
            source(e), tok.at[sender], send.at[k], recv.at[k], (s, sender), MESH
        )

    for k in range(1, n_exp):
        copy(k).start()
    own.start()
    own.wait()
    for k in range(1, n_exp):
        arriving(k).wait_recv()
    square = jnp.zeros((rows, 1), jnp.float32)
    for j in range(n_exp):
        cols = pl.ds(j * width, width)
        hid = (
            res_ref[:, cols].astype(jnp.float32)
            + tok[j].astype(jnp.float32) * again_ref[:, cols]
        ).astype(jnp.bfloat16)
        hid_ref[:, cols] = hid
        wide = hid.astype(jnp.float32)
        square = square + jnp.sum(wide * wide, axis=1, keepdims=True)
    scale = lax.rsqrt(square / (n_exp * width) + 1e-06)
    for j in range(n_exp):
        cols = pl.ds(j * width, width)
        in_ref[:, cols] = (
            hid_ref[:, cols].astype(jnp.float32) * scale * mgain_ref[:, cols]
        ).astype(jnp.bfloat16)
    for k in range(1, n_exp):
        copy(k).wait_send()


def mix_tokens(normed, residual, attn_gain, moe_gain, n_exp):
    vmem = pl.BlockSpec(memory_space=pltpu.VMEM)
    return pl.pallas_call(
        functools.partial(mix_kernel, n_exp),
        out_shape=(jax.ShapeDtypeStruct(residual.shape, jnp.bfloat16),) * 2,
        in_specs=[vmem] * 4,
        out_specs=(vmem, vmem),
        scratch_shapes=[
            pltpu.VMEM((n_exp, residual.shape[0], normed.shape[1]), jnp.bfloat16),
            pltpu.SemaphoreType.DMA((n_exp,)),
            pltpu.SemaphoreType.DMA((n_exp,)),
            pltpu.SemaphoreType.DMA((1,)),
        ],
        compiler_params=pltpu.CompilerParams(collective_id=4, has_side_effects=True),
    )(normed, residual, attn_gain[None, :], moe_gain[None, :])


def body(
    queries,
    keys,
    values,
    log_decay,
    residual,
    attn_gain,
    moe_gain,
    expert_ids,
    gate_weights,
    w_gate,
    w_up,
    w_down,
):
    rows = queries.shape[0]
    heads = log_decay.shape[1]
    head_dim = queries.shape[1] // heads
    q_heads = queries.reshape(rows, heads, head_dim)
    k_heads = keys.reshape(rows, heads, head_dim)
    v_heads = values.reshape(rows, heads, head_dim)
    log_cum = jnp.cumsum(log_decay, axis=0)
    block_total = log_cum[-1]
    keys_weighted = (k_heads * jnp.exp(block_total[None, :] - log_cum)[:, :, None]).astype(
        jnp.bfloat16
    )
    block_state = jnp.einsum(
        "thd,the->hde", keys_weighted, v_heads, preferred_element_type=jnp.float32
    )
    carried = carried_in(block_total, block_state, lax.axis_size("seq"))
    scores = jnp.einsum("thd,shd->hts", q_heads, k_heads, preferred_element_type=jnp.float32)
    gap_logs = log_cum.T[:, :, None] - log_cum.T[:, None, :]
    causal_mask = (
        lax.broadcasted_iota(jnp.int32, (rows, rows), 0)
        >= lax.broadcasted_iota(jnp.int32, (rows, rows), 1)
    )[None, :, :]
    weights = jnp.where(
        causal_mask, scores * jnp.exp(jnp.where(causal_mask, gap_logs, 0.0)), 0.0
    ).astype(jnp.bfloat16)
    intra = jnp.einsum("hts,she->the", weights, v_heads, preferred_element_type=jnp.float32)
    inter = jnp.exp(log_cum)[:, :, None] * jnp.einsum(
        "thd,hde->the", q_heads.astype(jnp.float32), carried, precision=lax.Precision.HIGHEST
    )
    attn = intra + inter
    normed = (attn * lax.rsqrt(jnp.mean(attn * attn, axis=-1, keepdims=True) + 1e-06)).astype(
        jnp.bfloat16
    )
    normed = normed.reshape(rows, heads * head_dim)
    hidden, moe_in = mix_tokens(normed, residual, attn_gain, moe_gain, lax.axis_size("exp"))
    hid32 = hidden.astype(jnp.float32)
    n_seq, n_exp = lax.axis_size("seq"), lax.axis_size("exp")
    tok_rows = residual.shape[0]
    experts = w_gate.shape[0] * n_exp
    gates = jnp.sum(
        jnp.where(
            expert_ids[:, :, None] == jnp.arange(experts, dtype=jnp.int32)[None, None, :],
            gate_weights[:, :, None],
            0.0,
        ),
        axis=1,
    )
    flat = gates.T.reshape(-1)
    pad = -flat.shape[0] % 1024
    g_tile = jnp.pad(flat, (0, pad)).reshape(-1, 128)
    everyone, g_all = gather_all(moe_in, g_tile, n_seq, n_exp)
    g_all = g_all.reshape(n_seq * n_exp, -1)[:, : experts * tok_rows]
    g_all = g_all.reshape(n_seq * n_exp, experts, tok_rows)
    mixed = None
    gate_col = lax.dynamic_slice_in_dim(
        g_all, lax.axis_index("exp") * w_gate.shape[0], w_gate.shape[0], 1
    )
    part = None
    for j in range(w_gate.shape[0]):
        gate_part = jnp.einsum("td,fd->tf", everyone, w_gate[j], preferred_element_type=jnp.float32)
        up_part = jnp.einsum("td,fd->tf", everyone, w_up[j], preferred_element_type=jnp.float32)
        active = (
            jax.nn.silu(gate_part) * up_part * gate_col[:, j, :].reshape(-1, 1)
        ).astype(jnp.bfloat16)
        one = jnp.dot(active, w_down[j], preferred_element_type=jnp.float32)
        part = one if part is None else part + one
    part = part.astype(jnp.bfloat16)
    total_rows, width = part.shape
    pieces = max(1, total_rows // 1024)
    step = width // pieces
    summed = [
        jax.jit(scatter_sum, static_argnums=(1, 2))(part[:, i * step : (i + 1) * step], n_seq, n_exp) for i in range(pieces)
    ]
    summed = summed[0] if pieces == 1 else jnp.concatenate(summed, axis=1)
    return (hid32 + summed).astype(jnp.bfloat16)


def solution(mesh):
    in_specs = (
        P("seq", "exp"),
        P("seq", "exp"),
        P("seq", "exp"),
        P("seq", "exp"),
        P(("seq", "exp"), None),
        P(),
        P(),
        P(("seq", "exp"), None),
        P(("seq", "exp"), None),
        P("exp", "seq", None),
        P("exp", "seq", None),
        P("exp", "seq", None),
    )
    out_specs = P(("seq", "exp"), None)
    return jax.shard_map(body, mesh=mesh, in_specs=in_specs, out_specs=out_specs, check_vma=False)
```

profile of v0, /device:TPU:8, one launch (start us, length us, event | category | flops | bytes accessed | tf_op | source)
XLA Modules:
  0.0 175.1 jit_solution(5685898525199806058)
XLA Ops:
  0.0 0.0 copy-start
  0.0 0.8 select_reduce_fusion
  0.8 0.1 reshape.70
  0.8 0.6 pad_bitcast_fusion.g_ref
  1.5 0.8 copy.26
  2.2 0.2 reduce_window_sum.11
  2.4 0.7 broadcast_in_dim.53.tot_ref
  3.2 0.1 copy.32
  3.3 1.1 copy.38
  4.4 0.0 copy-done
  4.5 1.1 fusion.43
  5.6 15.4 %shard_map.118 = f32[8,128,128]{2,1,0:T(8,128)} custom-call(f32[8,128,128]{2,1,0:T(8,128)} %get-tuple-element.16.own_ref, bf16[8,128,128]{2,1,0:T(8,128)(2,1)} %get-tuple-element.15.own16_ref, f32[8,128]{1,0:T(8,128)} %broadcast_in_dim.53.tot_ref), custom_call_target="tpu_custom_call" | custom-call | tf_op jit(solution)/shard_map/pallas_call | solution.py:504
  21.0 1.7 fusion.20
  22.7 1.5 multiply_reduce_fusion
  24.2 0.9 copy.39.normed_ref
  25.0 7.1 %shard_map.119 = (bf16[32,4096]{1,0:T(8,128)(2,1)}, bf16[32,4096]{1,0:T(8,128)(2,1)}) custom-call(bf16[128,1024]{1,0:T(8,128)(2,1)} %copy.39.normed_ref, bf16[32,4096]{1,0:T(8,128)(2,1)} %res_ref.1, f32[1,4096]{1,0:T(1,128)} %bitcast.76, f32[1,4096]{1,0:T(1,128)} %bitcast.77), custom_call_target="tpu_custom_call" | custom-call | tf_op jit(solution)/shard_map/pallas_call | solution.py:578
  32.1 47.4 %shard_map.120 = (bf16[1024,4096]{1,0:T(8,128)(2,1)}, f32[256,128]{1,0:T(8,128)}) custom-call(bf16[32,4096]{1,0:T(8,128)(2,1)} %get-tuple-element.10.x_ref, f32[8,128]{1,0:T(8,128)} %pad_bitcast_fusion.g_ref), custom_call_target="tpu_custom_call" | custom-call | tf_op jit(solution)/shard_map/pallas_call | solution.py:236
  79.5 0.9 reshape.72
  80.5 0.1 reshape.73
  80.6 0.1 dynamic-slice_reduce_fusion
  80.6 0.1 mul.57
  80.7 0.0 slice-start
  80.7 0.0 slice-start.1
  80.7 17.8 %fusion.4 = f32[1024,1152]{1,0:T(8,128)} fusion(bf16[1024,4096]{1,0:T(8,128)(2,1)} %get-tuple-element.11, bf16[1,1152,4096]{2,1,0:T(8,128)(2,1)} %param.21), kind=kOutput, calls=%fused_computation.4 | convolution fusion | flops 9663676416 | bytes 22544384 | tf_op jit(solution)/shard_map/td,fd->tf/dot_general | solution.py:665
  98.5 0.0 slice-start.2
  98.5 17.0 %fusion.15 = bf16[1024,1152]{1,0:T(8,128)(2,1)S(1)} fusion(bf16[1024,4096]{1,0:T(8,128)(2,1)} %get-tuple-element.11, bf16[1,1152,4096]{2,1,0:T(8,128)(2,1)} %param.22, f32[1024,1152]{1,0:T(8,128)} %fusion.4, f32[1024]{0:T(1024)S(1)} %mul.57), kind=kOutput, calls=%fused_computation.9 | convolution fusion | flops 9671933952 | bytes 24907776 | tf_op jit(solution)/shard_map/td,fd->tf/dot_general | solution.py:666
  115.5 0.0 slice-done
  115.5 0.0 slice-done.1
  115.5 0.0 slice-done.2
  115.5 13.0 %fusion.6.y_ref = bf16[1024,4096]{1,0:T(8,128)(2,1)} fusion(bf16[1024,1152]{1,0:T(8,128)(2,1)S(1)} %fusion.15, bf16[1,1152,4096]{2,1,0:T(8,128)(2,1)S(1)} %bitcast.80), kind=kOutput, calls=%fused_computation.6 | convolution fusion | flops 9667870720 | bytes 20185088 | tf_op jit(solution)/shard_map/dot_general | solution.py:670
  128.5 0.0 copy-start.1
  128.5 44.7 %scatter_sum.1 = f32[32,4096]{1,0:T(8,128)} custom-call(bf16[1024,4096]{1,0:T(8,128)(2,1)} %fusion.6.y_ref), custom_call_target="tpu_custom_call" | custom-call | tf_op jit(solution)/shard_map/jit(scatter_sum)/pallas_call | solution.py:398
  173.3 0.0 copy-done.1
  173.3 1.8 %add_convert_fusion = bf16[32,4096]{1,0:T(8,128)(2,1)} fusion(f32[32,4096]{1,0:T(8,128)} %scatter_sum.1, bf16[32,4096]{1,0:T(8,128)(2,1)S(1)} %copy-done.1), kind=kLoop, calls=%fused_computation.17 | loop fusion | flops 393216 | bytes 1048576 | tf_op jit(solution)/shard_map/convert_element_type | solution.py:680
  (9 shorter events, 0.2 us)
Async XLA Ops:
  0.0 4.4 %copy-start = (bf16[128,1024]{1,0:T(8,128)(2,1)S(1)}, bf16[128,1024]{1,0:T(8,128)(2,1)}, u32[]{:S(2)}) copy-start(bf16[128,1024]{1,0:T(8,128)(2,1)} %param.14) | copy-start | bytes 786436
  80.7 34.8 %slice-start = ((s8[9437184]{0:T(1024)(128)(4,1)}), s8[1048576]{0:T(1024)(128)(4,1)S(1)}, s32[]{:S(2)}) async-start(s8[9437184]{0:T(1024)(128)(4,1)} %bitcast.79), calls=%async_computation | async-start | bytes 2097152
  80.7 34.8 %slice-start.1 = ((s8[9437184]{0:T(1024)(128)(4,1)}), s8[4194304]{0:T(1024)(128)(4,1)S(1)}, s32[]{:S(2)}) async-start(s8[9437184]{0:T(1024)(128)(4,1)} %bitcast.79), calls=%async_computation.1 | async-start | bytes 8388608
  98.5 17.0 %slice-start.2 = ((s8[9437184]{0:T(1024)(128)(4,1)}), s8[4194304]{0:T(1024)(128)(4,1)S(1)}, s32[]{:S(2)}) async-start(s8[9437184]{0:T(1024)(128)(4,1)} %bitcast.79), calls=%async_computation.2 | async-start | bytes 8388608
  128.5 44.8 %copy-start.1 = (bf16[32,4096]{1,0:T(8,128)(2,1)S(1)}, bf16[32,4096]{1,0:T(8,128)(2,1)}, u32[]{:S(2)}) copy-start(bf16[32,4096]{1,0:T(8,128)(2,1)} %get-tuple-element.9) | copy-start | bytes 786436
where the time goes:
time: 178 us; the launch traced here: 175 us
  Pallas kernels  115 us (65%)
  matrix products  52 us (29%)
  local copies, waits for them, and re-layouts  5.46 us (3%)
  other arithmetic  2.83 us (2%)
    pallas_call x1, Pallas kernels, gather_all(): pl.pallas_call(functools.partial(gather_kernel, n_seq, n_exp), out_shape=...  47.4 us
    pallas_call x1, Pallas kernels, scatter_sum(): pl.pallas_call(functools.partial(scatter_kernel, n_seq, n_exp), out_shape...  44.7 us
    dot_general x1, matrix products, body(): jnp.einsum('td,fd->tf', everyone, w_gate[j], preferred_element_type=jnp.f...  17.8 us
    dot_general x1, matrix products, body(): jnp.einsum('td,fd->tf', everyone, w_up[j], preferred_element_type=jnp.flo...  17 us
    pallas_call x1, Pallas kernels, carried_in(): pl.pallas_call(functools.partial(carry_kernel, n_seq), out_shape=jax.Shap...  15.4 us
    dot_general x1, matrix products, body(): one = jnp.dot(active, w_down[j], preferred_element_type=jnp.float32)  13 us
    pallas_call x1, Pallas kernels, mix_tokens(): pl.pallas_call(functools.partial(mix_kernel, n_exp), out_shape=(jax.Shape...  7.08 us

commit v1 on v0

--- a/solution.py
+++ b/solution.py
@@ -418,6 +418,450 @@
     )(part)
 
 
+GPARTS = 2
+HPARTS = 4
+
+
+def plane_orders(length):
+    visit = []
+    for p in range(length):
+        visit.append(sorted(range(length), key=lambda q: (abs(q - p), q)))
+    lines = []
+    for p in range(length):
+        def ready(q):
+            chain = range(0, p + 1) if q > p else range(p, length)
+            return max(visit[b].index(q) for b in chain)
+
+        low = 2 * p < length
+        lines.append(sorted((q for q in range(length) if q != p), key=lambda q: (ready(q), -q if low else q)))
+    return visit, lines
+
+
+def pick(table, p, j):
+    total = 0
+    for a, row in enumerate(table):
+        for b, v in enumerate(row):
+            hit = jnp.logical_and(p == a, j == b).astype(jnp.int32)
+            total = total + hit * v
+    return total
+
+
+def spans(tiles, parts):
+    cuts = [(tiles * i // parts) * 128 for i in range(parts + 1)]
+    return [pl.ds(a, b - a) for a, b in zip(cuts[:-1], cuts[1:])]
+
+
+def when(cond, fn):
+    def run():
+        fn()
+
+    pl.when(cond)(run)
+
+
+def moe_kernel(
+    n_seq, n_exp, x_ref, hid_ref, wg_ref, wu_ref, wd_ref, out_ref,
+    xs, ys, act, sib, din, xin, yin, lin, tot, wg, wu, wd,
+    gsend, grecv, bsend, brecv, ssend, srecv, loc,
+):
+    me = Place(n_seq, n_exp)
+    L, p = me.length, me.p
+    rows, width = out_ref.shape
+    hidden = wg.shape[0]
+    many = 8 * rows
+    f32, bf = jnp.float32, jnp.bfloat16
+    X, Y, C = me.dev(dx=1), me.dev(dy=1), me.dev(dc=1)
+    visit, lines = plane_orders(L)
+    gcols = spans(x_ref.shape[1] // 128, GPARTS)
+    hcols = spans(width // 128, HPARTS)
+
+    loads = [
+        pltpu.make_async_copy(a.at[0], b, loc.at[i])
+        for i, (a, b) in enumerate(((wg_ref, wg), (wu_ref, wu), (wd_ref, wd)))
+    ]
+    for cp in loads:
+        cp.start()
+
+    def flip(v, d):
+        return 1 - v if d else v
+
+    def row(q, dx=0, dy=0, dc=0):
+        k = (flip(me.c, dc) * 2 + flip(me.x, dx)) * 2 + flip(me.y, dy)
+        return pl.ds(pl.multiple_of((q * 8 + k) * rows, rows), rows)
+
+    def srow(q, dx=0, dy=0):
+        k = flip(me.x, dx) * 2 + flip(me.y, dy)
+        return pl.ds(pl.multiple_of((q * 4 + k) * rows, rows), rows)
+
+    def prow(q):
+        return pl.ds(pl.multiple_of(q * rows, rows), rows)
+
+    def gcopy(kind, q, part, r, to, skind=None):
+        ref = xs.at[r, gcols[part]]
+        skind = kind if skind is None else skind
+        return pltpu.make_async_remote_copy(
+            ref, ref, gsend.at[skind, q, part], grecv.at[kind, q, part], to, MESH
+        )
+
+    upper = GPARTS // 2
+
+    def line_pair(q, part, do):
+        pl.when(jnp.logical_and(q >= p, p > 0))(
+            lambda: do(gcopy(0, q, part, row(q), me.dev(dp=-1)))
+        )
+        pl.when(jnp.logical_and(q <= p, p + 1 < L))(
+            lambda: do(gcopy(0, q, part, row(q), me.dev(dp=1), 9))
+        )
+
+    def start(cp):
+        cp.start()
+
+    def g_line(q, part):
+        pl.when(q != p)(lambda: gcopy(0, q, part, row(q), X).wait_recv())
+        line_pair(q, part, start)
+
+    def first(q, part):
+        return [gcopy(1, q, part, row(q), X), gcopy(2, q, part, row(q), Y), gcopy(5, q, part, row(q), C)]
+
+    def second_x(q, part):
+        out = [gcopy(6, q, part, row(q, 1, 0), C)]
+        return out if part >= upper else [gcopy(3, q, part, row(q, 1, 0), Y)] + out
+
+    def second_y(q, part):
+        out = [gcopy(7, q, part, row(q, 0, 1), C)]
+        return out if part < upper else [gcopy(4, q, part, row(q, 0, 1), X)] + out
+
+    def third(q, part):
+        return [gcopy(8, q, part, row(q, 1, 1), C)]
+
+    def g_first(q, part):
+        for cp in first(q, part):
+            cp.start()
+
+    def g_second(q, part):
+        gcopy(1, q, part, row(q, 1, 0), X).wait_recv()
+        for cp in second_x(q, part):
+            cp.start()
+        gcopy(2, q, part, row(q, 0, 1), X).wait_recv()
+        for cp in second_y(q, part):
+            cp.start()
+
+    def g_third(q, part):
+        gcopy(3 if part < upper else 4, q, part, row(q, 1, 1), X).wait_recv()
+        for cp in third(q, part):
+            cp.start()
+
+    def g_done(q):
+        for part in range(GPARTS):
+            gcopy(5, q, part, row(q, 0, 0, 1), X).wait_recv()
+            gcopy(6, q, part, row(q, 1, 0, 1), X).wait_recv()
+            gcopy(7, q, part, row(q, 0, 1, 1), X).wait_recv()
+            gcopy(8, q, part, row(q, 1, 1, 1), X).wait_recv()
+
+    def g_drain(q):
+        for part in range(GPARTS):
+            line_pair(q, part, lambda cp: cp.wait_send())
+            for cp in first(q, part) + second_x(q, part) + second_y(q, part) + third(q, part):
+                cp.wait_send()
+
+    def sib_copy(q, h):
+        r = pl.ds(pl.multiple_of((q * 2 + 1 - me.c) * 4 * rows, 4 * rows), 4 * rows)
+        d = pl.ds(pl.multiple_of(q * 4 * rows, 4 * rows), 4 * rows)
+        return pltpu.make_async_remote_copy(
+            ys.at[r, hcols[h]], sib.at[d, hcols[h]], bsend.at[q, h], brecv.at[q, h], C, MESH
+        )
+
+    def scopy(kind, q, h, r, dst, d, to):
+        return pltpu.make_async_remote_copy(
+            ys.at[r, hcols[h]], dst.at[d, hcols[h]], ssend.at[kind, q, h], srecv.at[kind, q, h], to, MESH
+        )
+
+    def diag_copy(q, h):
+        return scopy(0, q, h, row(q, 1, 1), din, prow(q), Y if 2 * h < HPARTS else X)
+
+    def x_copy(q, h):
+        return scopy(1, q, h, row(q, 1, 0), xin, prow(q), X)
+
+    def y_copy(q, h):
+        return scopy(2, q, h, row(q, 0, 1), yin, prow(q), Y)
+
+    def line_copy(q, h):
+        up = (q > p).astype(jnp.int32)
+        last = jnp.logical_and(q < p, q == p - 1).astype(jnp.int32)
+        slot = q + (L - q) * last
+        return pltpu.make_async_remote_copy(
+            ys.at[row(q), hcols[h]],
+            lin.at[prow(slot), hcols[h]],
+            ssend.at[3, q, h],
+            srecv.at[3, slot, h],
+            me.dev(dp=2 * up - 1),
+            MESH,
+        )
+
+    def line_in(slot, h):
+        return pltpu.make_async_remote_copy(
+            ys.at[row(p), hcols[h]], lin.at[prow(slot), hcols[h]], ssend.at[3, p, h], srecv.at[3, slot, h], X, MESH
+        )
+
+    def pair(q, h, dx, dy):
+        return ys[row(q, dx, dy), hcols[h]].astype(f32) + sib[srow(q, dx, dy), hcols[h]].astype(f32)
+
+    def r_first(q, h):
+        sib_copy(q, h).wait_recv()
+        ys[row(q, 1, 1), hcols[h]] = pair(q, h, 1, 1).astype(bf)
+        diag_copy(q, h).start()
+
+    def r_second(q, h):
+        sx, sy = pair(q, h, 1, 0), pair(q, h, 0, 1)
+        diag_copy(q, h).wait_recv()
+        more = din[prow(q), hcols[h]].astype(f32)
+        if 2 * h < HPARTS:
+            sx = sx + more
+        else:
+            sy = sy + more
+        ys[row(q, 1, 0), hcols[h]] = sx.astype(bf)
+        x_copy(q, h).start()
+        ys[row(q, 0, 1), hcols[h]] = sy.astype(bf)
+        y_copy(q, h).start()
+
+    def r_third(q, h):
+        total = pair(q, h, 0, 0)
+        x_copy(q, h).wait_recv()
+        y_copy(q, h).wait_recv()
+        total = total + xin[prow(q), hcols[h]].astype(f32) + yin[prow(q), hcols[h]].astype(f32)
+        tot[prow(q), hcols[h]] = total
+
+    def r_line(q, h):
+        behind = jnp.logical_or(jnp.logical_and(q > p, p > 0), jnp.logical_and(q < p, p < L - 1))
+
+        @pl.when(behind)
+        def _():
+            line_in(q, h).wait_recv()
+            ys[row(q), hcols[h]] = (tot[prow(q), hcols[h]] + lin[prow(q), hcols[h]].astype(f32)).astype(bf)
+
+        @pl.when(jnp.logical_not(behind))
+        def _():
+            ys[row(q), hcols[h]] = tot[prow(q), hcols[h]].astype(bf)
+
+        line_copy(q, h).start()
+
+    def r_last(h):
+        cols = hcols[h]
+
+        @pl.when(p > 0)
+        def _():
+            line_in(p, h).wait_recv()
+            tot[prow(p), cols] += lin[prow(p), cols].astype(f32)
+
+        @pl.when(p < L - 1)
+        def _():
+            line_in(L, h).wait_recv()
+            tot[prow(p), cols] += lin[prow(L), cols].astype(f32)
+
+        out_ref[:, cols] = (hid_ref[:, cols].astype(f32) + tot[prow(p), cols]).astype(bf)
+
+    at_end = jnp.logical_or(p == 0, p == L - 1)
+
+    def r_early(q, h):
+        pl.when(jnp.logical_and(at_end, q != p))(lambda: r_line(q, h))
+
+    def r_drain(q):
+        for h in range(HPARTS):
+            sib_copy(q, h).wait_send()
+            diag_copy(q, h).wait_send()
+            x_copy(q, h).wait_send()
+            y_copy(q, h).wait_send()
+            pl.when(q != p)(lambda: line_copy(q, h).wait_send())
+
+    tile = next(t for t in range(512, 0, -128) if hidden % t == 0)
+    fsteps = hidden // tile
+
+    def block_of(q):
+        return pl.ds(pl.multiple_of(q * many, many), many)
+
+    def gate_of(q):
+        extra = xs[block_of(q), width : width + 128].astype(f32)
+        lane = lax.broadcasted_iota(jnp.int32, extra.shape, 1)
+        e = lax.axis_index("exp")
+        keep = jnp.logical_or(lane == e, lane == e + 64)
+        return jnp.sum(jnp.where(keep, extra, 0.0), axis=1, keepdims=True)
+
+    nt = (((1,), (1,)), ((), ()))
+
+    def ffn_in(q, f):
+        fc = pl.ds(f * tile, tile)
+        rows_in = xs[block_of(q), 0:width]
+        gate = lax.dot_general(rows_in, wg[fc, :], nt, preferred_element_type=f32)
+        up = lax.dot_general(rows_in, wu[fc, :], nt, preferred_element_type=f32)
+        act[:, fc] = (gate / (1.0 + jnp.exp(-gate)) * up * gate_of(q)).astype(bf)
+
+    def ffn_out(q, h):
+        ys[block_of(q), hcols[h]] = jnp.dot(
+            act[...], wd[:, hcols[h]], preferred_element_type=f32
+        ).astype(bf)
+        sib_copy(q, h).start()
+
+    me.greet()
+    xs[row(p), :] = x_ref[...]
+    plane = [pick(visit, p, j) for j in range(min(3, L))]
+    for part in range(GPARTS):
+        g_line(plane[0], part)
+        g_first(plane[0], part)
+    for part in range(GPARTS):
+        g_second(plane[0], part)
+        if L > 1:
+            g_line(plane[1], part)
+            g_first(plane[1], part)
+    for part in range(GPARTS):
+        g_third(plane[0], part)
+    if L > 2:
+        for part in range(GPARTS):
+            g_line(plane[2], part)
+            g_first(plane[2], part)
+    for cp in loads:
+        cp.wait()
+
+    def chunk(j, carry):
+        q, nxt, prev = pick(visit, p, j), pick(visit, p, j + 1), pick(visit, p, j - 1)
+        far = pick(visit, p, j + 3)
+
+        def ahead(fn):
+            when(j + 1 < L, fn)
+
+        def after(fn):
+            when(j > 0, fn)
+
+        def hook(n):
+            if n == 0:
+                after(lambda: (r_second(prev, 0), r_second(prev, 1)))
+                ahead(lambda: g_second(nxt, 0))
+            if n == 1:
+                after(lambda: (r_second(prev, 2), r_second(prev, 3)))
+                ahead(lambda: [g_second(nxt, part) for part in range(1, GPARTS)])
+
+                @pl.when(j + 3 < L)
+                def _():
+                    for part in range(GPARTS):
+                        g_line(far, part)
+                        g_first(far, part)
+
+            if n == 2:
+                after(lambda: (r_third(prev, 0), r_early(prev, 0), r_third(prev, 1), r_early(prev, 1)))
+                ahead(lambda: [g_third(nxt, part) for part in range(GPARTS)])
+
+        g_done(q)
+        after(lambda: r_first(prev, HPARTS - 1))
+        for f in range(fsteps):
+            ffn_in(q, f)
+            hook(f)
+        for f in range(fsteps, 3):
+            hook(f)
+        for h in range(HPARTS):
+            ffn_out(q, h)
+            if h:
+                r_first(q, h - 1)
+            if h == 1:
+                after(lambda: (r_third(prev, 2), r_early(prev, 2)))
+            if h == 2:
+                after(lambda: (r_third(prev, 3), r_early(prev, 3)))
+        return carry
+
+    lax.fori_loop(0, L, chunk, 0)
+
+    final = pick(visit, p, L - 1)
+    inner = jnp.logical_not(at_end)
+    r_first(final, HPARTS - 1)
+    for h in range(HPARTS):
+        r_second(final, h)
+
+    def one_line(i, hs):
+        q = pick(lines, p, i)
+
+        @pl.when(inner)
+        def _():
+            for h in hs:
+                r_line(q, h)
+
+    if L > 2:
+        one_line(0, range(HPARTS))
+    for h in range(HPARTS):
+        r_third(final, h)
+        r_early(final, h)
+    for i in range(1, L - 1):
+        one_line(i, range(HPARTS))
+    for h in range(HPARTS):
+        r_last(h)
+
+    def drain(q, carry):
+        g_drain(q)
+        r_drain(q)
+        return carry
+
+    lax.fori_loop(0, L, drain, 0)
+
+
+def moe_scratch(n_seq, n_exp, x_shape, w_shape):
+    n, L = n_seq * n_exp, n_seq * n_exp // 8
+    rows, wide = x_shape
+    hidden, width = w_shape[1:]
+    bf, f32 = jnp.bfloat16, jnp.float32
+    return [
+        ((n * rows, wide), bf),
+        ((n * rows, width), bf),
+        ((8 * rows, hidden), bf),
+        ((n // 2 * rows, width), bf),
+        ((L * rows, width), bf),
+        ((L * rows, width), bf),
+        ((L * rows, width), bf),
+        ((L * rows + rows, width), bf),
+        ((L * rows, width), f32),
+        ((hidden, width), bf),
+        ((hidden, width), bf),
+        ((hidden, width), bf),
+    ]
+
+
+MOE_VMEM = 60 * 2**20
+
+
+def moe_fits(n_seq, n_exp, x_shape, w_shape):
+    need = sum(a * b * jnp.dtype(t).itemsize for (a, b), t in moe_scratch(n_seq, n_exp, x_shape, w_shape))
+    return (
+        w_shape[0] == 1
+        and n_exp <= 64
+        and w_shape[1] % 128 == 0
+        and w_shape[2] % (128 * HPARTS) == 0
+        and need + 5 * 2**20 <= MOE_VMEM
+    )
+
+
+def moe_layer(x, hid, w_gate, w_up, w_down, n_seq, n_exp):
+    L = n_seq * n_exp // 8
+    vmem = pl.BlockSpec(memory_space=pltpu.VMEM)
+    anyspace = pl.BlockSpec(memory_space=pl.ANY)
+    dma = pltpu.SemaphoreType.DMA
+    return pl.pallas_call(
+        functools.partial(moe_kernel, n_seq, n_exp),
+        out_shape=jax.ShapeDtypeStruct(hid.shape, jnp.bfloat16),
+        in_specs=[vmem, vmem, anyspace, anyspace, anyspace],
+        out_specs=vmem,
+        scratch_shapes=[
+            pltpu.VMEM(s, t) for s, t in moe_scratch(n_seq, n_exp, x.shape, w_gate.shape)
+        ]
+        + [
+            dma((10, L, GPARTS)),
+            dma((10, L, GPARTS)),
+            dma((L, HPARTS)),
+            dma((L, HPARTS)),
+            dma((4, L + 1, HPARTS)),
+            dma((4, L + 1, HPARTS)),
+            dma((3,)),
+        ],
+        compiler_params=pltpu.CompilerParams(
+            collective_id=5, has_side_effects=True, vmem_limit_bytes=MOE_VMEM
+        ),
+    )(x, hid, w_gate, w_up, w_down)
+
+
 def carry_kernel(n_seq, own_ref, own16_ref, tot_ref, out_ref, peer, ptot, cin, cout, send, recv, tsem):
     s, e = lax.axis_index("seq"), lax.axis_index("exp")
     z, odd, deep = s // 2, s % 2, n_seq // 2
@@ -519,7 +963,7 @@
     )(block_state, block_state.astype(bf), tile)
 
 
-def mix_kernel(n_exp, normed_ref, res_ref, again_ref, mgain_ref, hid_ref, in_ref, tok, send, recv, loc):
+def mix_kernel(n_exp, normed_ref, res_ref, again_ref, mgain_ref, tile_ref, hid_ref, in_ref, tok, send, recv, loc):
     s, e = lax.axis_index("seq"), lax.axis_index("exp")
     rows, width = res_ref.shape[0], normed_ref.shape[1]
 
@@ -553,6 +997,7 @@
     own.wait()
     for k in range(1, n_exp):
         arriving(k).wait_recv()
+    in_ref[:, n_exp * width :] = tile_ref[...]
     square = jnp.zeros((rows, 1), jnp.float32)
     for j in range(n_exp):
         cols = pl.ds(j * width, width)
@@ -573,12 +1018,17 @@
         copy(k).wait_send()
 
 
-def mix_tokens(normed, residual, attn_gain, moe_gain, n_exp):
+def mix_tokens(normed, residual, attn_gain, moe_gain, tile, n_exp):
     vmem = pl.BlockSpec(memory_space=pltpu.VMEM)
     return pl.pallas_call(
         functools.partial(mix_kernel, n_exp),
-        out_shape=(jax.ShapeDtypeStruct(residual.shape, jnp.bfloat16),) * 2,
-        in_specs=[vmem] * 4,
+        out_shape=(
+            jax.ShapeDtypeStruct(residual.shape, jnp.bfloat16),
+            jax.ShapeDtypeStruct(
+                (residual.shape[0], residual.shape[1] + tile.shape[1]), jnp.bfloat16
+            ),
+        ),
+        in_specs=[vmem] * 5,
         out_specs=(vmem, vmem),
         scratch_shapes=[
             pltpu.VMEM((n_exp, residual.shape[0], normed.shape[1]), jnp.bfloat16),
@@ -587,7 +1037,7 @@
             pltpu.SemaphoreType.DMA((1,)),
         ],
         compiler_params=pltpu.CompilerParams(collective_id=4, has_side_effects=True),
-    )(normed, residual, attn_gain[None, :], moe_gain[None, :])
+    )(normed, residual, attn_gain[None, :], moe_gain[None, :], tile)
 
 
 def body(
@@ -610,7 +1060,11 @@
     q_heads = queries.reshape(rows, heads, head_dim)
     k_heads = keys.reshape(rows, heads, head_dim)
     v_heads = values.reshape(rows, heads, head_dim)
-    log_cum = jnp.cumsum(log_decay, axis=0)
+    upto = (
+        lax.broadcasted_iota(jnp.int32, (rows, rows), 0)
+        >= lax.broadcasted_iota(jnp.int32, (rows, rows), 1)
+    ).astype(jnp.float32)
+    log_cum = jnp.dot(upto, log_decay, precision=lax.Precision.HIGHEST)
     block_total = log_cum[-1]
     keys_weighted = (k_heads * jnp.exp(block_total[None, :] - log_cum)[:, :, None]).astype(
         jnp.bfloat16
@@ -637,10 +1091,8 @@
         jnp.bfloat16
     )
     normed = normed.reshape(rows, heads * head_dim)
-    hidden, moe_in = mix_tokens(normed, residual, attn_gain, moe_gain, lax.axis_size("exp"))
-    hid32 = hidden.astype(jnp.float32)
     n_seq, n_exp = lax.axis_size("seq"), lax.axis_size("exp")
-    tok_rows = residual.shape[0]
+    tok_rows, width = residual.shape
     experts = w_gate.shape[0] * n_exp
     gates = jnp.sum(
         jnp.where(
@@ -650,6 +1102,19 @@
         ),
         axis=1,
     )
+    if experts <= 64:
+        coarse = lax.reduce_precision(gates, 8, 7)
+        spare = ((0, 0), (0, 64 - experts))
+        tile = jnp.concatenate([jnp.pad(coarse, spare), jnp.pad(gates - coarse, spare)], axis=1)
+    else:
+        tile = jnp.zeros((tok_rows, 128), jnp.float32)
+    hidden, moe_in = mix_tokens(
+        normed, residual, attn_gain, moe_gain, tile.astype(jnp.bfloat16), n_exp
+    )
+    if moe_fits(n_seq, n_exp, moe_in.shape, w_gate.shape):
+        return moe_layer(moe_in, hidden, w_gate, w_up, w_down, n_seq, n_exp)
+    moe_in = moe_in[:, :width]
+    hid32 = hidden.astype(jnp.float32)
     flat = gates.T.reshape(-1)
     pad = -flat.shape[0] % 1024
     g_tile = jnp.pad(flat, (0, pad)).reshape(-1, 128)

time: 178 us -> 151 us (0.85)
  the two profiles are of different devices: /device:TPU:8 before, /device:TPU:0 now
where the time goes in v1:
time: 151 us
  Pallas kernels  139 us (92%)
  matrix products  5.1 us (3%)
  local copies, waits for them, and re-layouts  4.74 us (3%)
  other arithmetic  1.54 us (1%)
    pallas_call x1, Pallas kernels, moe_layer(): pl.pallas_call(functools.partial(moe_kernel, n_seq, n_exp), out_shape=jax...  118 us
    pallas_call x1, Pallas kernels, carried_in(): pl.pallas_call(functools.partial(carry_kernel, n_seq), out_shape=jax.Shap...  14.5 us
    pallas_call x1, Pallas kernels, mix_tokens(): pl.pallas_call(functools.partial(mix_kernel, n_exp), out_shape=(jax.Shape...  7.08 us

profile of v1, /device:TPU:0, one launch (start us, length us, event | category | flops | bytes accessed | tf_op | source)
XLA Modules:
  0.0 150.6 jit_solution(4532990911772482557)
XLA Ops:
  0.0 0.0 copy-start
  0.0 0.8 fusion.23
  0.9 0.2 slice_reduce_fusion
  1.1 0.1 fusion.29
  1.2 1.1 copy.52
  2.3 0.0 copy-done
  2.3 1.1 fusion.30
  3.4 0.7 broadcast_in_dim.53.tot_ref
  4.1 14.5 %shard_map.118 = f32[8,128,128]{2,1,0:T(8,128)} custom-call(f32[8,128,128]{2,1,0:T(8,128)} %get-tuple-element.14.own_ref, bf16[8,128,128]{2,1,0:T(8,128)(2,1)} %get-tuple-element.13.own16_ref, f32[8,128]{1,0:T(8,128)} %broadcast_in_dim.53.tot_ref), custom_call_target="tpu_custom_call" | custom-call | tf_op jit(solution)/shard_map/pallas_call | solution.py:948
  18.6 1.7 %fusion.2 = f32[128,8,128]{0,2,1:T(8,128)S(1)} fusion(f32[8,128,128]{2,1,0:T(8,128)} %shard_map.118, f32[128,8]{0,1:T(8,128)S(1)} %get-tuple-element.11, bf16[128,1024]{1,0:T(8,128)(2,1)} %param.12), kind=kOutput, calls=%fused_computation.5 | convolution fusion | flops 201457664 | bytes 1314816 | tf_op jit(solution)/shard_map/thd,hde->the/dot_general | solution.py:1086
  20.3 1.4 multiply_reduce_fusion
  21.8 0.9 copy.51.normed_ref
  22.7 0.7 select_reduce_fusion
  23.4 0.1 copy.47
  23.5 0.1 copy.48
  23.6 0.7 fusion.26.tile_ref
  24.2 7.1 %shard_map.119 = (bf16[32,4096]{1,0:T(8,128)(2,1)}, bf16[32,4224]{1,0:T(8,128)(2,1)}) custom-call(bf16[128,1024]{1,0:T(8,128)(2,1)} %copy.51.normed_ref, bf16[32,4096]{1,0:T(8,128)(2,1)} %res_ref.1, f32[1,4096]{1,0:T(1,128)} %bitcast.51, f32[1,4096]{1,0:T(1,128)} %bitcast.52, bf16[32,128]{1,0:T(8,128)(2,1)} %fusion.26.tile_ref), custom_call_target="tpu_custom_call" | custom-call | tf_op jit(solution)/shard_map/pallas_call | solution.py:1023
  31.3 117.6 %shard_map.120 = bf16[32,4096]{1,0:T(8,128)(2,1)} custom-call(bf16[32,4224]{1,0:T(8,128)(2,1)} %get-tuple-element.7.x_ref, bf16[32,4096]{1,0:T(8,128)(2,1)} %get-tuple-element.8.hid_ref, bf16[1,1152,4096]{2,1,0:T(8,128)(2,1)} %wg_ref.1, bf16[1,1152,4096]{2,1,0:T(8,128)(2,1)} %wu_ref.1, bf16[1,1152,4096]{2,1,0:T(8,128)(2,1)} %wd_ref.1), custom_call_target="tpu_custom_call" | custom-call | tf_op jit(solution)/shard_map/pallas_call | solution.py:842
  149.0 1.7 %copy.79 = bf16[32,4096]{1,0:T(8,128)(2,1)} copy(bf16[32,4096]{1,0:T(8,128)(2,1)} %shard_map.120) | data formatting | bytes 524288
  (5 shorter events, 0.1 us)
Async XLA Ops:
  0.0 2.3 %copy-start = (bf16[128,1024]{1,0:T(8,128)(2,1)S(1)}, bf16[128,1024]{1,0:T(8,128)(2,1)}, u32[]{:S(2)}) copy-start(bf16[128,1024]{1,0:T(8,128)(2,1)} %param.14) | copy-start | bytes 786436

commit v2 on v1

--- a/solution.py
+++ b/solution.py
@@ -32,9 +32,9 @@
         c = 1 - self.c if dc else self.c
         return self.ids(self.p + dp, x, y, c)
 
-    def greet(self):
+    def greet(self, *more):
         barrier = pltpu.get_barrier_semaphore()
-        for d in (dict(dx=1), dict(dy=1), dict(dc=1)):
+        for d in (dict(dx=1), dict(dy=1), dict(dc=1), *more):
             pl.semaphore_signal(barrier, inc=1, device_id=self.dev(**d), device_id_type=MESH)
 
         @pl.when(self.p > 0)
@@ -46,7 +46,7 @@
             pl.semaphore_signal(barrier, inc=1, device_id=self.dev(dp=1), device_id_type=MESH)
 
         ends = (self.p > 0).astype(jnp.int32) + (self.p < self.length - 1).astype(jnp.int32)
-        pl.semaphore_wait(barrier, 3 + ends)
+        pl.semaphore_wait(barrier, 3 + len(more) + ends)
 
     def at(self, stage, sign, k):
         if sign == 0:
@@ -418,14 +418,21 @@
     )(part)
 
 
-GPARTS = 2
+GPARTS = 4
 HPARTS = 4
+PLANES = 4
 
 
 def plane_orders(length):
+    def depth(q):
+        return min(q, length - 1 - q)
+
     visit = []
     for p in range(length):
-        visit.append(sorted(range(length), key=lambda q: (abs(q - p), q)))
+        rest = [q for q in range(length) if q != p]
+        near = min(rest, key=lambda q: (abs(q - p), depth(q)), default=p)
+        rest = sorted((q for q in rest if q != near), key=lambda q: (depth(q), abs(q - p)))
+        visit.append([p] + [near] * (length > 1) + rest)
     lines = []
     for p in range(length):
         def ready(q):
@@ -458,10 +465,160 @@
     pl.when(cond)(run)
 
 
+def attend_tokens(
+    me, q_ref, k_ref, v_ref, ld_ref, res_ref, ag_ref, mg_ref, tile_ref, x_out,
+    hid, work, flat, own16, peer, cin, cout, tots, tok, psend, precv, tsem, msend, mrecv,
+):
+    L, z = me.length, me.p
+    f32, bf = jnp.float32, jnp.bfloat16
+    block, heads = ld_ref.shape
+    dim = q_ref.shape[1] // heads
+    rows = res_ref.shape[0]
+    n_exp, width = tok.shape[0], tok.shape[2]
+    e = lax.axis_index("exp")
+    pair = me.dev(dx=1)
+
+    def head(h):
+        return pl.ds(h * dim, dim)
+
+    def pair_copy(h):
+        return pltpu.make_async_remote_copy(
+            own16.at[h], peer.at[h], psend.at[0, h], precv.at[0, h], pair, MESH
+        )
+
+    def line_copy(h):
+        return pltpu.make_async_remote_copy(
+            cout.at[h], cin.at[h], psend.at[1, h], precv.at[1, h], me.dev(dp=1), MESH
+        )
+
+    tot_copy = pltpu.make_async_remote_copy(tots.at[0], tots.at[1], tsem.at[0], tsem.at[1], pair, MESH)
+
+    nt = (((1,), (1,)), ((), ()))
+    tn = (((0,), (0,)), ((), ()))
+    r = lax.broadcasted_iota(jnp.int32, (block, block), 0)
+    c = lax.broadcasted_iota(jnp.int32, (block, block), 1)
+    seen = r >= c
+    decay = ld_ref[...]
+    high = lax.Precision.HIGHEST
+    cum = jnp.dot(seen.astype(f32), decay, precision=high, preferred_element_type=f32)
+    cum_t = lax.dot_general(decay, (r <= c).astype(f32), tn, precision=high, preferred_element_type=f32)
+    total = cum_t[:, block - 1 :]
+    tots[0, 0:heads, :] = jnp.broadcast_to(total, (heads, dim))
+
+    def state(h):
+        kw = (k_ref[:, head(h)].astype(f32) * jnp.exp(total[h : h + 1] - cum[:, h : h + 1])).astype(bf)
+        own = lax.dot_general(kw, v_ref[:, head(h)], tn, preferred_element_type=f32)
+        work[:, pl.ds((heads + h) * dim, dim)] = own
+        own16[h] = own.astype(bf)
+
+    for h in range(heads):
+        state(h)
+    me.greet(dict(dy=1, dc=1))
+    tot_copy.start()
+    for h in range(heads):
+        pair_copy(h).start()
+
+    @pl.when(z == 0)
+    def _():
+        cin[...] = jnp.zeros_like(cin)
+
+    for h in range(heads):
+        scores = lax.dot_general(q_ref[:, head(h)], k_ref[:, head(h)], nt, preferred_element_type=f32)
+        gap = cum[:, h : h + 1] - cum_t[h : h + 1, :]
+        weights = jnp.where(seen, scores * jnp.exp(jnp.where(seen, gap, 0.0)), 0.0).astype(bf)
+        work[:, head(h)] = jnp.dot(weights, v_ref[:, head(h)], preferred_element_type=f32)
+
+    tot_copy.wait_recv()
+    mine, other = tots[0, 0:heads, :], tots[1, 0:heads, :]
+    both = jnp.exp(mine + other)
+    is_odd = jnp.full(mine.shape, me.x, jnp.int32) == 1
+    one = jnp.ones_like(mine)
+    own_by = jnp.where(is_odd, one, jnp.exp(other))
+    peer_by = jnp.where(is_odd, jnp.exp(mine), one)
+    carry_by = jnp.where(is_odd, jnp.exp(other), one)
+    peer_in = jnp.where(is_odd, one, jnp.zeros_like(mine))
+
+    peers = (dict(dc=1), dict(dy=1), dict(dy=1, dc=1))
+    pieces = 2
+    span = width // pieces
+
+    def mix_copy(k, i):
+        to = me.dev(**peers[k])
+        cols = pl.ds(i * span, span)
+        src = flat.at[pl.ds(pl.multiple_of(to[1] * rows, rows), rows), cols]
+        return pltpu.make_async_remote_copy(
+            src, tok.at[e, :, cols], msend.at[k, i], mrecv.at[k, i], to, MESH
+        )
+
+    def mix_in(k, i):
+        to = me.dev(**peers[k])
+        cols = pl.ds(i * span, span)
+        return pltpu.make_async_remote_copy(
+            tok.at[to[1], :, cols], tok.at[to[1], :, cols], msend.at[k, i], mrecv.at[k, i], to, MESH
+        )
+
+    for h in range(heads):
+        pair_copy(h).wait_recv()
+        pl.when(z > 0)(lambda: line_copy(h).wait_recv())
+        near = peer[h].astype(f32)
+        come = cin[h].astype(f32)
+        row = slice(h, h + 1)
+
+        @pl.when(z < L - 1)
+        def _():
+            mix = both[row] * come + own_by[row] * work[:, pl.ds((heads + h) * dim, dim)] + peer_by[row] * near
+            cout[h] = mix.astype(bf)
+            line_copy(h).start()
+
+        carried = carry_by[row] * come + peer_in[row] * near
+        coarse = carried.astype(bf)
+        fine = (carried - coarse.astype(f32)).astype(bf)
+        query = q_ref[:, head(h)]
+        inter = jnp.dot(query, coarse, preferred_element_type=f32) + jnp.dot(
+            query, fine, preferred_element_type=f32
+        )
+        attn = work[:, head(h)] + jnp.exp(cum[:, h : h + 1]) * inter
+        scale = lax.rsqrt(jnp.mean(attn * attn, axis=-1, keepdims=True) + 1e-06)
+        flat[0:block, head(h)] = (attn * scale).astype(bf)
+        if (h + 1) * pieces % heads == 0:
+            for k in range(len(peers)):
+                mix_copy(k, (h + 1) * pieces // heads - 1).start()
+
+    tok[e] = flat[pl.ds(pl.multiple_of(e * rows, rows), rows), 0:width]
+    for i in range(pieces):
+        for k in range(len(peers)):
+            mix_in(k, i).wait_recv()
+    square = jnp.zeros((rows, 1), f32)
+    for j in range(n_exp):
+        cols = pl.ds(j * width, width)
+        value = (res_ref[:, cols].astype(f32) + tok[j].astype(f32) * ag_ref[:, cols]).astype(bf)
+        hid[:, cols] = value
+        wide = value.astype(f32)
+        square = square + jnp.sum(wide * wide, axis=1, keepdims=True)
+    scale = lax.rsqrt(square / (n_exp * width) + 1e-06)
+    for j in range(n_exp):
+        cols = pl.ds(j * width, width)
+        x_out[:, cols] = (hid[:, cols].astype(f32) * scale * mg_ref[:, cols]).astype(bf)
+    x_out[:, n_exp * width :] = tile_ref[...]
+
+    def finish():
+        tot_copy.wait_send()
+        for h in range(heads):
+            pair_copy(h).wait_send()
+            pl.when(z < L - 1)(lambda: line_copy(h).wait_send())
+        for i in range(pieces):
+            for k in range(len(peers)):
+                mix_copy(k, i).wait_send()
+
+    return finish
+
+
 def moe_kernel(
-    n_seq, n_exp, x_ref, hid_ref, wg_ref, wu_ref, wd_ref, out_ref,
-    xs, ys, act, sib, din, xin, yin, lin, tot, wg, wu, wd,
-    gsend, grecv, bsend, brecv, ssend, srecv, loc,
+    n_seq, n_exp, q_ref, k_ref, v_ref, ld_ref, res_ref, ag_ref, mg_ref, tile_ref,
+    wg_ref, wu_ref, wd_ref, out_ref,
+    xs, ys, act, sib, din, xin, yin, lin, tot, wg, wu, wd, hid_ref,
+    own16, peer, cin, cout, tots, tok,
+    gsend, grecv, bsend, brecv, ssend, srecv, loc, psend, precv, tsem, msend, mrecv,
 ):
     me = Place(n_seq, n_exp)
     L, p = me.length, me.p
@@ -471,7 +628,7 @@
     f32, bf = jnp.float32, jnp.bfloat16
     X, Y, C = me.dev(dx=1), me.dev(dy=1), me.dev(dc=1)
     visit, lines = plane_orders(L)
-    gcols = spans(x_ref.shape[1] // 128, GPARTS)
+    gcols = spans(xs.shape[1] // 128, GPARTS)
     hcols = spans(width // 128, HPARTS)
 
     loads = [
@@ -520,7 +677,7 @@
         line_pair(q, part, start)
 
     def first(q, part):
-        return [gcopy(1, q, part, row(q), X), gcopy(2, q, part, row(q), Y), gcopy(5, q, part, row(q), C)]
+        return [gcopy(2, q, part, row(q), Y), gcopy(5, q, part, row(q), C)]
 
     def second_x(q, part):
         out = [gcopy(6, q, part, row(q, 1, 0), C)]
@@ -533,22 +690,57 @@
     def third(q, part):
         return [gcopy(8, q, part, row(q, 1, 1), C)]
 
-    def g_first(q, part):
-        for cp in first(q, part):
-            cp.start()
-
-    def g_second(q, part):
+    lower, higher = range(upper), range(upper, GPARTS)
+
+    def g_first(q, turn):
+        for part in lower if turn == 0 else higher:
+            gcopy(1, q, part, row(q), X).start()
+        for part in higher if turn == 0 else lower:
+            gcopy(2, q, part, row(q), Y).start()
+        if turn == 0:
+            for part in range(GPARTS):
+                gcopy(5, q, part, row(q), C).start()
+
+    def g_own(q):
+        for part in lower:
+            line_pair(q, part, start)
+        g_first(q, 0)
+        for part in lower:
+            gcopy(1, q, part, row(q), X).wait_send()
+        for part in higher:
+            line_pair(q, part, start)
+        g_first(q, 1)
+
+    def from_x(q, part):
         gcopy(1, q, part, row(q, 1, 0), X).wait_recv()
         for cp in second_x(q, part):
             cp.start()
+
+    def from_y(q, part):
         gcopy(2, q, part, row(q, 0, 1), X).wait_recv()
         for cp in second_y(q, part):
             cp.start()
 
-    def g_third(q, part):
-        gcopy(3 if part < upper else 4, q, part, row(q, 1, 1), X).wait_recv()
-        for cp in third(q, part):
-            cp.start()
+    def g_second(q):
+        for part in lower:
+            from_x(q, part)
+            from_y(q, part + upper)
+
+    def g_rest(q):
+        for part in lower:
+            from_x(q, part + upper)
+            from_y(q, part)
+
+    def g_third(q):
+        for part in range(GPARTS):
+            gcopy(3 if part < upper else 4, q, part, row(q, 1, 1), X).wait_recv()
+            for cp in third(q, part):
+                cp.start()
+
+    def g_ring(k, parts):
+        for sign in (-1, 1):
+            q = p + sign * k
+            when(jnp.logical_and(q >= 0, q < L), lambda: [g_line(q, part) for part in parts])
 
     def g_done(q):
         for part in range(GPARTS):
@@ -560,6 +752,11 @@
     def g_drain(q):
         for part in range(GPARTS):
             line_pair(q, part, lambda cp: cp.wait_send())
+            across = gcopy(1, q, part, row(q), X)
+            if part < upper:
+                pl.when(q != p)(lambda: across.wait_send())
+            else:
+                across.wait_send()
             for cp in first(q, part) + second_x(q, part) + second_y(q, part) + third(q, part):
                 cp.wait_send()
 
@@ -660,6 +857,7 @@
         out_ref[:, cols] = (hid_ref[:, cols].astype(f32) + tot[prow(p), cols]).astype(bf)
 
     at_end = jnp.logical_or(p == 0, p == L - 1)
+    inner = jnp.logical_not(at_end)
 
     def r_early(q, h):
         pl.when(jnp.logical_and(at_end, q != p))(lambda: r_line(q, h))
@@ -700,29 +898,26 @@
         ).astype(bf)
         sib_copy(q, h).start()
 
-    me.greet()
-    xs[row(p), :] = x_ref[...]
-    plane = [pick(visit, p, j) for j in range(min(3, L))]
-    for part in range(GPARTS):
-        g_line(plane[0], part)
-        g_first(plane[0], part)
-    for part in range(GPARTS):
-        g_second(plane[0], part)
-        if L > 1:
-            g_line(plane[1], part)
-            g_first(plane[1], part)
-    for part in range(GPARTS):
-        g_third(plane[0], part)
-    if L > 2:
-        for part in range(GPARTS):
-            g_line(plane[2], part)
-            g_first(plane[2], part)
+    front_done = attend_tokens(
+        me, q_ref, k_ref, v_ref, ld_ref, res_ref, ag_ref, mg_ref, tile_ref, xs.at[row(p)],
+        hid_ref, tot, act, own16, peer, cin, cout, tots, tok, psend, precv, tsem, msend, mrecv,
+    )
+    second = pick(visit, p, 1)
+    g_own(p)
+    g_second(p)
+    g_ring(1, lower)
+    g_rest(p)
+    g_ring(1, higher)
+    g_first(second, 0)
+    g_third(p)
+    g_ring(2, lower)
+    g_first(second, 1)
+    front_done()
     for cp in loads:
         cp.wait()
 
     def chunk(j, carry):
         q, nxt, prev = pick(visit, p, j), pick(visit, p, j + 1), pick(visit, p, j - 1)
-        far = pick(visit, p, j + 3)
 
         def ahead(fn):
             when(j + 1 < L, fn)
@@ -730,23 +925,27 @@
         def after(fn):
             when(j > 0, fn)
 
+        def opening(fn):
+            when(j == 0, fn)
+
+        def closing(fn):
+            when(j == L - 1, fn)
+
         def hook(n):
             if n == 0:
+                opening(lambda: g_ring(2, higher))
                 after(lambda: (r_second(prev, 0), r_second(prev, 1)))
-                ahead(lambda: g_second(nxt, 0))
+                ahead(lambda: g_second(nxt))
+                opening(lambda: when(inner, lambda: g_first(pick(visit, p, 2), 0)))
             if n == 1:
                 after(lambda: (r_second(prev, 2), r_second(prev, 3)))
-                ahead(lambda: [g_second(nxt, part) for part in range(1, GPARTS)])
-
-                @pl.when(j + 3 < L)
-                def _():
-                    for part in range(GPARTS):
-                        g_line(far, part)
-                        g_first(far, part)
-
+                ahead(lambda: g_rest(nxt))
+                opening(lambda: g_ring(3, range(GPARTS)))
+                opening(lambda: when(at_end, lambda: g_first(pick(visit, p, 2), 0)))
+                opening(lambda: g_first(pick(visit, p, 2), 1))
             if n == 2:
+                opening(lambda: g_first(pick(visit, p, 3), 0))
                 after(lambda: (r_third(prev, 0), r_early(prev, 0), r_third(prev, 1), r_early(prev, 1)))
-                ahead(lambda: [g_third(nxt, part) for part in range(GPARTS)])
 
         g_done(q)
         after(lambda: r_first(prev, HPARTS - 1))
@@ -760,36 +959,32 @@
             if h:
                 r_first(q, h - 1)
             if h == 1:
-                after(lambda: (r_third(prev, 2), r_early(prev, 2)))
+                after(lambda: (r_third(prev, 2), r_early(prev, 2), r_third(prev, 3), r_early(prev, 3)))
             if h == 2:
-                after(lambda: (r_third(prev, 3), r_early(prev, 3)))
+                ahead(lambda: g_third(nxt))
+            if h == 3:
+                opening(lambda: g_first(pick(visit, p, 3), 1))
         return carry
 
+    def one_line(i, h):
+        when(inner, lambda: r_line(pick(lines, p, i), h))
+
     lax.fori_loop(0, L, chunk, 0)
 
     final = pick(visit, p, L - 1)
-    inner = jnp.logical_not(at_end)
     r_first(final, HPARTS - 1)
     for h in range(HPARTS):
         r_second(final, h)
-
-    def one_line(i, hs):
-        q = pick(lines, p, i)
-
-        @pl.when(inner)
-        def _():
-            for h in hs:
-                r_line(q, h)
-
-    if L > 2:
-        one_line(0, range(HPARTS))
+        one_line(0, h)
     for h in range(HPARTS):
+        one_line(1, h)
         r_third(final, h)
         r_early(final, h)
-    for i in range(1, L - 1):
-        one_line(i, range(HPARTS))
     for h in range(HPARTS):
-        r_last(h)
+        one_line(2, h)
+        if h:
+            r_last(h - 1)
+    r_last(HPARTS - 1)
 
     def drain(q, carry):
         g_drain(q)
@@ -820,34 +1015,51 @@
     ]
 
 
-MOE_VMEM = 60 * 2**20
-
-
-def moe_fits(n_seq, n_exp, x_shape, w_shape):
-    need = sum(a * b * jnp.dtype(t).itemsize for (a, b), t in moe_scratch(n_seq, n_exp, x_shape, w_shape))
+MOE_VMEM = 61 * 2**20
+
+
+def moe_fits(n_seq, n_exp, rows, width, w_shape):
+    need = sum(
+        a * b * jnp.dtype(t).itemsize for (a, b), t in moe_scratch(n_seq, n_exp, (rows, width + 128), w_shape)
+    )
     return (
         w_shape[0] == 1
-        and n_exp <= 64
+        and n_exp // 4 == 1
+        and n_seq * n_exp == 8 * PLANES
         and w_shape[1] % 128 == 0
         and w_shape[2] % (128 * HPARTS) == 0
-        and need + 5 * 2**20 <= MOE_VMEM
+        and need + 6 * 2**20 <= MOE_VMEM
     )
 
 
-def moe_layer(x, hid, w_gate, w_up, w_down, n_seq, n_exp):
+def whole_layer(
+    queries, keys, values, log_decay, residual, attn_gain, moe_gain, tile, w_gate, w_up, w_down, n_seq, n_exp
+):
     L = n_seq * n_exp // 8
+    heads = log_decay.shape[1]
+    part = queries.shape[1]
+    dim = part // heads
+    rows, width = residual.shape
     vmem = pl.BlockSpec(memory_space=pltpu.VMEM)
     anyspace = pl.BlockSpec(memory_space=pl.ANY)
     dma = pltpu.SemaphoreType.DMA
+    bf = jnp.bfloat16
+    states = pltpu.VMEM((heads, dim, dim), bf)
+    scratch = moe_scratch(n_seq, n_exp, (rows, width + tile.shape[1]), w_gate.shape)
     return pl.pallas_call(
         functools.partial(moe_kernel, n_seq, n_exp),
-        out_shape=jax.ShapeDtypeStruct(hid.shape, jnp.bfloat16),
-        in_specs=[vmem, vmem, anyspace, anyspace, anyspace],
+        out_shape=jax.ShapeDtypeStruct(residual.shape, bf),
+        in_specs=[vmem] * 8 + [anyspace] * 3,
         out_specs=vmem,
-        scratch_shapes=[
-            pltpu.VMEM(s, t) for s, t in moe_scratch(n_seq, n_exp, x.shape, w_gate.shape)
-        ]
+        scratch_shapes=[pltpu.VMEM(s, t) for s, t in scratch]
         + [
+            pltpu.VMEM(residual.shape, bf),
+            states,
+            states,
+            states,
+            states,
+            pltpu.VMEM((2, heads + -heads % 8, dim), jnp.float32),
+            pltpu.VMEM((n_exp, rows, part), bf),
             dma((10, L, GPARTS)),
             dma((10, L, GPARTS)),
             dma((L, HPARTS)),
@@ -855,11 +1067,19 @@
             dma((4, L + 1, HPARTS)),
             dma((4, L + 1, HPARTS)),
             dma((3,)),
+            dma((2, heads)),
+            dma((2, heads)),
+            dma((2,)),
+            dma((3, 2)),
+            dma((3, 2)),
         ],
         compiler_params=pltpu.CompilerParams(
             collective_id=5, has_side_effects=True, vmem_limit_bytes=MOE_VMEM
         ),
-    )(x, hid, w_gate, w_up, w_down)
+    )(
+        queries, keys, values, log_decay, residual, attn_gain[None, :], moe_gain[None, :], tile,
+        w_gate, w_up, w_down,
+    )
 
 
 def carry_kernel(n_seq, own_ref, own16_ref, tot_ref, out_ref, peer, ptot, cin, cout, send, recv, tsem):
@@ -963,7 +1183,7 @@
     )(block_state, block_state.astype(bf), tile)
 
 
-def mix_kernel(n_exp, normed_ref, res_ref, again_ref, mgain_ref, tile_ref, hid_ref, in_ref, tok, send, recv, loc):
+def mix_kernel(n_exp, normed_ref, res_ref, again_ref, mgain_ref, hid_ref, in_ref, tok, send, recv, loc):
     s, e = lax.axis_index("seq"), lax.axis_index("exp")
     rows, width = res_ref.shape[0], normed_ref.shape[1]
 
@@ -997,7 +1217,6 @@
     own.wait()
     for k in range(1, n_exp):
         arriving(k).wait_recv()
-    in_ref[:, n_exp * width :] = tile_ref[...]
     square = jnp.zeros((rows, 1), jnp.float32)
     for j in range(n_exp):
         cols = pl.ds(j * width, width)
@@ -1018,17 +1237,12 @@
         copy(k).wait_send()
 
 
-def mix_tokens(normed, residual, attn_gain, moe_gain, tile, n_exp):
+def mix_tokens(normed, residual, attn_gain, moe_gain, n_exp):
     vmem = pl.BlockSpec(memory_space=pltpu.VMEM)
     return pl.pallas_call(
         functools.partial(mix_kernel, n_exp),
-        out_shape=(
-            jax.ShapeDtypeStruct(residual.shape, jnp.bfloat16),
-            jax.ShapeDtypeStruct(
-                (residual.shape[0], residual.shape[1] + tile.shape[1]), jnp.bfloat16
-            ),
-        ),
-        in_specs=[vmem] * 5,
+        out_shape=(jax.ShapeDtypeStruct(residual.shape, jnp.bfloat16),) * 2,
+        in_specs=[vmem] * 4,
         out_specs=(vmem, vmem),
         scratch_shapes=[
             pltpu.VMEM((n_exp, residual.shape[0], normed.shape[1]), jnp.bfloat16),
@@ -1037,7 +1251,7 @@
             pltpu.SemaphoreType.DMA((1,)),
         ],
         compiler_params=pltpu.CompilerParams(collective_id=4, has_side_effects=True),
-    )(normed, residual, attn_gain[None, :], moe_gain[None, :], tile)
+    )(normed, residual, attn_gain[None, :], moe_gain[None, :])
 
 
 def body(
@@ -1054,6 +1268,25 @@
     w_up,
     w_down,
 ):
+    n_seq, n_exp = lax.axis_size("seq"), lax.axis_size("exp")
+    tok_rows, width = residual.shape
+    experts = w_gate.shape[0] * n_exp
+    gates = jnp.sum(
+        jnp.where(
+            expert_ids[:, :, None] == jnp.arange(experts, dtype=jnp.int32)[None, None, :],
+            gate_weights[:, :, None],
+            0.0,
+        ),
+        axis=1,
+    )
+    if moe_fits(n_seq, n_exp, tok_rows, width, w_gate.shape):
+        coarse = lax.reduce_precision(gates, 8, 7)
+        spare = ((0, 0), (0, 64 - experts))
+        tile = jnp.concatenate([jnp.pad(coarse, spare), jnp.pad(gates - coarse, spare)], axis=1)
+        return whole_layer(
+            queries, keys, values, log_decay, residual, attn_gain, moe_gain,
+            tile.astype(jnp.bfloat16), w_gate, w_up, w_down, n_seq, n_exp,
+        )
     rows = queries.shape[0]
     heads = log_decay.shape[1]
     head_dim = queries.shape[1] // heads
@@ -1091,29 +1324,7 @@
         jnp.bfloat16
     )
     normed = normed.reshape(rows, heads * head_dim)
-    n_seq, n_exp = lax.axis_size("seq"), lax.axis_size("exp")
-    tok_rows, width = residual.shape
-    experts = w_gate.shape[0] * n_exp
-    gates = jnp.sum(
-        jnp.where(
-            expert_ids[:, :, None] == jnp.arange(experts, dtype=jnp.int32)[None, None, :],
-            gate_weights[:, :, None],
-            0.0,
-        ),
-        axis=1,
-    )
-    if experts <= 64:
-        coarse = lax.reduce_precision(gates, 8, 7)
-        spare = ((0, 0), (0, 64 - experts))
-        tile = jnp.concatenate([jnp.pad(coarse, spare), jnp.pad(gates - coarse, spare)], axis=1)
-    else:
-        tile = jnp.zeros((tok_rows, 128), jnp.float32)
-    hidden, moe_in = mix_tokens(
-        normed, residual, attn_gain, moe_gain, tile.astype(jnp.bfloat16), n_exp
-    )
-    if moe_fits(n_seq, n_exp, moe_in.shape, w_gate.shape):
-        return moe_layer(moe_in, hidden, w_gate, w_up, w_down, n_seq, n_exp)
-    moe_in = moe_in[:, :width]
+    hidden, moe_in = mix_tokens(normed, residual, attn_gain, moe_gain, n_exp)
     hid32 = hidden.astype(jnp.float32)
     flat = gates.T.reshape(-1)
     pad = -flat.shape[0] % 1024

time: 151 us -> 127 us (0.84)
  the two profiles are of different devices: /device:TPU:0 before, /device:TPU:8 now
where the time goes in v2:
time: 127 us; the launch traced here: 126 us
  Pallas kernels  122 us (96%)
  local copies, waits for them, and re-layouts  3.26 us (3%)
  other arithmetic  1.39 us (1%)
    pallas_call x1, Pallas kernels, whole_layer(): pl.pallas_call(functools.partial(moe_kernel, n_seq, n_exp), out_shape=jax...  122 us
    unnamed x2, local copies, waits for them, and re-layouts  3.08 us

profile of v2, /device:TPU:8, one launch (start us, length us, event | category | flops | bytes accessed | tf_op | source)
XLA Modules:
  0.0 126.4 jit_solution(1262931068468204109)
XLA Ops:
  0.0 0.7 select_reduce_fusion
  0.7 0.1 copy.20
  0.8 0.1 copy.19
  0.9 0.7 fusion.2.tile_ref
  1.6 1.4 %copy.22.ld_ref = f32[128,8]{1,0:T(8,128)} copy(f32[128,8]{0,1:T(8,128)} %param.15) | data formatting | bytes 8192 | tf_op args[3]
  3.0 121.8 %shard_map.118 = bf16[32,4096]{1,0:T(8,128)(2,1)} custom-call(bf16[128,1024]{1,0:T(8,128)(2,1)} %q_ref.1, bf16[128,1024]{1,0:T(8,128)(2,1)} %k_ref.1, bf16[128,1024]{1,0:T(8,128)(2,1)} %v_ref.1, f32[128,8]{1,0:T(8,128)} %copy.22.ld_ref, bf16[32,4096]{1,0:T(8,128)(2,1)} %res_ref.1, f32[1,4096]{1,0:T(1,128)} %bitcast.2, f32[1,4096]{1,0:T(1,128)} %bitcast.3, ...), custom_call_target="tpu_custom_call" | custom-call | tf_op jit(solution)/shard_map/pallas_call | solution.py:1049
  124.8 1.7 %copy.24 = bf16[32,4096]{1,0:T(8,128)(2,1)} copy(bf16[32,4096]{1,0:T(8,128)(2,1)} %shard_map.118) | data formatting | bytes 524288
  (2 shorter events, 0.0 us)

commit v3 on v2

--- a/solution.py
+++ b/solution.py
@@ -466,12 +466,12 @@
 
 
 def attend_tokens(
-    me, q_ref, k_ref, v_ref, ld_ref, res_ref, ag_ref, mg_ref, tile_ref, x_out,
+    me, q_ref, k_ref, v_ref, ld_ref, res_ref, ag_ref, mg_ref, ids_ref, gw_ref, x_out,
     hid, work, flat, own16, peer, cin, cout, tots, tok, psend, precv, tsem, msend, mrecv,
 ):
     L, z = me.length, me.p
     f32, bf = jnp.float32, jnp.bfloat16
-    block, heads = ld_ref.shape
+    heads, block = ld_ref.shape
     dim = q_ref.shape[1] // heads
     rows = res_ref.shape[0]
     n_exp, width = tok.shape[0], tok.shape[2]
@@ -500,8 +500,8 @@
     seen = r >= c
     decay = ld_ref[...]
     high = lax.Precision.HIGHEST
-    cum = jnp.dot(seen.astype(f32), decay, precision=high, preferred_element_type=f32)
-    cum_t = lax.dot_general(decay, (r <= c).astype(f32), tn, precision=high, preferred_element_type=f32)
+    cum = lax.dot_general(seen.astype(f32), decay, nt, precision=high, preferred_element_type=f32)
+    cum_t = jnp.dot(decay, (r <= c).astype(f32), precision=high, preferred_element_type=f32)
     total = cum_t[:, block - 1 :]
     tots[0, 0:heads, :] = jnp.broadcast_to(total, (heads, dim))
 
@@ -522,12 +522,14 @@
     def _():
         cin[...] = jnp.zeros_like(cin)
 
-    for h in range(heads):
+    def f_intra(h):
         scores = lax.dot_general(q_ref[:, head(h)], k_ref[:, head(h)], nt, preferred_element_type=f32)
         gap = cum[:, h : h + 1] - cum_t[h : h + 1, :]
         weights = jnp.where(seen, scores * jnp.exp(jnp.where(seen, gap, 0.0)), 0.0).astype(bf)
         work[:, head(h)] = jnp.dot(weights, v_ref[:, head(h)], preferred_element_type=f32)
 
+    for h in range(heads):
+        f_intra(h)
     tot_copy.wait_recv()
     mine, other = tots[0, 0:heads, :], tots[1, 0:heads, :]
     both = jnp.exp(mine + other)
@@ -557,7 +559,7 @@
             tok.at[to[1], :, cols], tok.at[to[1], :, cols], msend.at[k, i], mrecv.at[k, i], to, MESH
         )
 
-    for h in range(heads):
+    def f_chain(h):
         pair_copy(h).wait_recv()
         pl.when(z > 0)(lambda: line_copy(h).wait_recv())
         near = peer[h].astype(f32)
@@ -570,6 +572,10 @@
             cout[h] = mix.astype(bf)
             line_copy(h).start()
 
+    def f_head(h):
+        near = peer[h].astype(f32)
+        come = cin[h].astype(f32)
+        row = slice(h, h + 1)
         carried = carry_by[row] * come + peer_in[row] * near
         coarse = carried.astype(bf)
         fine = (carried - coarse.astype(f32)).astype(bf)
@@ -584,10 +590,18 @@
             for k in range(len(peers)):
                 mix_copy(k, (h + 1) * pieces // heads - 1).start()
 
+    for h in range(heads):
+        f_chain(h)
+        f_head(h)
+
     tok[e] = flat[pl.ds(pl.multiple_of(e * rows, rows), rows), 0:width]
-    for i in range(pieces):
-        for k in range(len(peers)):
-            mix_in(k, i).wait_recv()
+
+    def f_mix():
+        for i in range(pieces):
+            for k in range(len(peers)):
+                mix_in(k, i).wait_recv()
+
+    f_mix()
     square = jnp.zeros((rows, 1), f32)
     for j in range(n_exp):
         cols = pl.ds(j * width, width)
@@ -599,7 +613,23 @@
     for j in range(n_exp):
         cols = pl.ds(j * width, width)
         x_out[:, cols] = (hid[:, cols].astype(f32) * scale * mg_ref[:, cols]).astype(bf)
-    x_out[:, n_exp * width :] = tile_ref[...]
+
+    def column(ref):
+        same = lax.broadcasted_iota(jnp.int32, (rows, rows), 0) == lax.broadcasted_iota(jnp.int32, (rows, rows), 1)
+        return lax.dot_general(
+            same.astype(f32), ref[...].astype(f32), nt, precision=high, preferred_element_type=f32
+        )
+
+    ids, gates = column(ids_ref).astype(jnp.int32), column(gw_ref)
+    coarse = gates.astype(bf).astype(f32)
+    rest = gates - coarse
+    lane = lax.broadcasted_iota(jnp.int32, (rows, 128), 1)
+    extra = jnp.zeros((rows, 128), f32)
+    for i in range(ids_ref.shape[0]):
+        who = ids[:, i : i + 1]
+        extra = jnp.where(lane == who, coarse[:, i : i + 1], extra)
+        extra = jnp.where(lane == who + 64, rest[:, i : i + 1], extra)
+    x_out[:, n_exp * width :] = extra.astype(bf)
 
     def finish():
         tot_copy.wait_send()
@@ -614,7 +644,7 @@
 
 
 def moe_kernel(
-    n_seq, n_exp, q_ref, k_ref, v_ref, ld_ref, res_ref, ag_ref, mg_ref, tile_ref,
+    n_seq, n_exp, q_ref, k_ref, v_ref, ld_ref, res_ref, ag_ref, mg_ref, ids_ref, gw_ref,
     wg_ref, wu_ref, wd_ref, out_ref,
     xs, ys, act, sib, din, xin, yin, lin, tot, wg, wu, wd, hid_ref,
     own16, peer, cin, cout, tots, tok,
@@ -899,7 +929,7 @@
         sib_copy(q, h).start()
 
     front_done = attend_tokens(
-        me, q_ref, k_ref, v_ref, ld_ref, res_ref, ag_ref, mg_ref, tile_ref, xs.at[row(p)],
+        me, q_ref, k_ref, v_ref, ld_ref, res_ref, ag_ref, mg_ref, ids_ref, gw_ref, xs.at[row(p)],
         hid_ref, tot, act, own16, peer, cin, cout, tots, tok, psend, precv, tsem, msend, mrecv,
     )
     second = pick(visit, p, 1)
@@ -910,7 +940,6 @@
     g_ring(1, higher)
     g_first(second, 0)
     g_third(p)
-    g_ring(2, lower)
     g_first(second, 1)
     front_done()
     for cp in loads:
@@ -918,37 +947,47 @@
 
     def chunk(j, carry):
         q, nxt, prev = pick(visit, p, j), pick(visit, p, j + 1), pick(visit, p, j - 1)
-
-        def ahead(fn):
-            when(j + 1 < L, fn)
-
-        def after(fn):
-            when(j > 0, fn)
-
-        def opening(fn):
-            when(j == 0, fn)
-
-        def closing(fn):
-            when(j == L - 1, fn)
+        older = pick(visit, p, j - 2)
+        third, fourth = pick(visit, p, 2), pick(visit, p, 3)
+
+        def opening(*fns):
+            when(j == 0, lambda: [fn() for fn in fns])
+
+        def closing(*fns):
+            when(j == L - 1, lambda: [fn() for fn in fns])
+
+        def ahead(*fns):
+            when(jnp.logical_and(j > 0, j + 1 < L), lambda: [fn() for fn in fns])
+
+        def after(*fns):
+            when(j > 0, lambda: [fn() for fn in fns])
+
+        def later(*fns):
+            when(j > 1, lambda: [fn() for fn in fns])
+
+        def settle(at, h):
+            r_third(at, h)
+            r_early(at, h)
 
         def hook(n):
             if n == 0:
-                opening(lambda: g_ring(2, higher))
-                after(lambda: (r_second(prev, 0), r_second(prev, 1)))
+                after(lambda: r_first(prev, 2), lambda: r_first(prev, 3))
+                opening(
+                    lambda: g_ring(2, lower),
+                    lambda: g_second(nxt),
+                    lambda: g_ring(2, higher),
+                    lambda: g_first(fourth, 0),
+                )
+            if n == 1:
+                opening(lambda: g_rest(nxt), lambda: g_first(fourth, 1))
                 ahead(lambda: g_second(nxt))
-                opening(lambda: when(inner, lambda: g_first(pick(visit, p, 2), 0)))
-            if n == 1:
-                after(lambda: (r_second(prev, 2), r_second(prev, 3)))
+                later(lambda: settle(older, 0), lambda: settle(older, 1))
+                after(lambda: r_second(prev, 0), lambda: r_second(prev, 1))
+            if n == 2:
                 ahead(lambda: g_rest(nxt))
-                opening(lambda: g_ring(3, range(GPARTS)))
-                opening(lambda: when(at_end, lambda: g_first(pick(visit, p, 2), 0)))
-                opening(lambda: g_first(pick(visit, p, 2), 1))
-            if n == 2:
-                opening(lambda: g_first(pick(visit, p, 3), 0))
-                after(lambda: (r_third(prev, 0), r_early(prev, 0), r_third(prev, 1), r_early(prev, 1)))
+                later(lambda: settle(older, 2), lambda: settle(older, 3))
 
         g_done(q)
-        after(lambda: r_first(prev, HPARTS - 1))
         for f in range(fsteps):
             ffn_in(q, f)
             hook(f)
@@ -956,14 +995,20 @@
             hook(f)
         for h in range(HPARTS):
             ffn_out(q, h)
-            if h:
-                r_first(q, h - 1)
+            if h == 0:
+                after(lambda: r_second(prev, 2))
             if h == 1:
-                after(lambda: (r_third(prev, 2), r_early(prev, 2), r_third(prev, 3), r_early(prev, 3)))
+                after(lambda: r_second(prev, 3))
+                opening(lambda: g_ring(3, range(GPARTS)), lambda: g_first(third, 0))
             if h == 2:
+                r_first(q, 0)
                 ahead(lambda: g_third(nxt))
+                opening(lambda: g_third(nxt))
+                closing(lambda: settle(prev, 0))
             if h == 3:
-                opening(lambda: g_first(pick(visit, p, 3), 1))
+                r_first(q, 1)
+                opening(lambda: g_first(third, 1))
+                closing(lambda: settle(prev, 1))
         return carry
 
     def one_line(i, h):
@@ -971,8 +1016,12 @@
 
     lax.fori_loop(0, L, chunk, 0)
 
-    final = pick(visit, p, L - 1)
-    r_first(final, HPARTS - 1)
+    final, prior = pick(visit, p, L - 1), pick(visit, p, L - 2)
+    r_first(final, 2)
+    r_first(final, 3)
+    for h in (2, 3):
+        r_third(prior, h)
+        r_early(prior, h)
     for h in range(HPARTS):
         r_second(final, h)
         one_line(0, h)
@@ -1033,7 +1082,8 @@
 
 
 def whole_layer(
-    queries, keys, values, log_decay, residual, attn_gain, moe_gain, tile, w_gate, w_up, w_down, n_seq, n_exp
+    queries, keys, values, log_decay, residual, attn_gain, moe_gain, expert_ids, gate_weights,
+    w_gate, w_up, w_down, n_seq, n_exp,
 ):
     L = n_seq * n_exp // 8
     heads = log_decay.shape[1]
@@ -1045,11 +1095,11 @@
     dma = pltpu.SemaphoreType.DMA
     bf = jnp.bfloat16
     states = pltpu.VMEM((heads, dim, dim), bf)
-    scratch = moe_scratch(n_seq, n_exp, (rows, width + tile.shape[1]), w_gate.shape)
+    scratch = moe_scratch(n_seq, n_exp, (rows, width + 128), w_gate.shape)
     return pl.pallas_call(
         functools.partial(moe_kernel, n_seq, n_exp),
         out_shape=jax.ShapeDtypeStruct(residual.shape, bf),
-        in_specs=[vmem] * 8 + [anyspace] * 3,
+        in_specs=[vmem] * 9 + [anyspace] * 3,
         out_specs=vmem,
         scratch_shapes=[pltpu.VMEM(s, t) for s, t in scratch]
         + [
@@ -1077,8 +1127,8 @@
             collective_id=5, has_side_effects=True, vmem_limit_bytes=MOE_VMEM
         ),
     )(
-        queries, keys, values, log_decay, residual, attn_gain[None, :], moe_gain[None, :], tile,
-        w_gate, w_up, w_down,
+        queries, keys, values, log_decay.T, residual, attn_gain[None, :], moe_gain[None, :],
+        expert_ids.T, gate_weights.T, w_gate, w_up, w_down,
     )
 
 
@@ -1269,6 +1319,11 @@
     w_down,
 ):
     n_seq, n_exp = lax.axis_size("seq"), lax.axis_size("exp")
+    if moe_fits(n_seq, n_exp, *residual.shape, w_gate.shape):
+        return whole_layer(
+            queries, keys, values, log_decay, residual, attn_gain, moe_gain, expert_ids, gate_weights,
+            w_gate, w_up, w_down, n_seq, n_exp,
+        )
     tok_rows, width = residual.shape
     experts = w_gate.shape[0] * n_exp
     gates = jnp.sum(
@@ -1279,14 +1334,6 @@
         ),
         axis=1,
     )
-    if moe_fits(n_seq, n_exp, tok_rows, width, w_gate.shape):
-        coarse = lax.reduce_precision(gates, 8, 7)
-        spare = ((0, 0), (0, 64 - experts))
-        tile = jnp.concatenate([jnp.pad(coarse, spare), jnp.pad(gates - coarse, spare)], axis=1)
-        return whole_layer(
-            queries, keys, values, log_decay, residual, attn_gain, moe_gain,
-            tile.astype(jnp.bfloat16), w_gate, w_up, w_down, n_seq, n_exp,
-        )
     rows = queries.shape[0]
     heads = log_decay.shape[1]
     head_dim = queries.shape[1] // heads

time: 127 us -> 114 us (0.90)
  Pallas kernels: 122 us -> 112 us
  local copies, waits for them, and re-layouts: 3.26 us -> 1.67 us
  other arithmetic: 1.39 us -> 0 us
    pallas_call x1, Pallas kernels: 122 us -> 112 us  [whole_layer(): pl.pallas_call(functools.partial(moe_kernel, n_seq, n_exp), out_shape=jax...]
    unnamed x2 -> x1, local copies, waits for them, and re-layouts: 3.08 us -> 1.67 us
where the time goes in v3:
time: 114 us; the launch traced here: 113 us
  Pallas kernels  112 us (98%)
  local copies, waits for them, and re-layouts  1.67 us (1%)
    pallas_call x1, Pallas kernels, whole_layer(): pl.pallas_call(functools.partial(moe_kernel, n_seq, n_exp), out_shape=jax...  112 us

profile of v3, /device:TPU:8, one launch (start us, length us, event | category | flops | bytes accessed | tf_op | source)
XLA Modules:
  0.0 113.4 jit_solution(7236451649946404492)
XLA Ops:
  0.0 111.7 %shard_map.118 = bf16[32,4096]{1,0:T(8,128)(2,1)} custom-call(bf16[128,1024]{1,0:T(8,128)(2,1)} %q_ref.1, bf16[128,1024]{1,0:T(8,128)(2,1)} %k_ref.1, bf16[128,1024]{1,0:T(8,128)(2,1)} %v_ref.1, f32[8,128]{1,0:T(8,128)} %bitcast.7, bf16[32,4096]{1,0:T(8,128)(2,1)} %res_ref.1, f32[1,4096]{1,0:T(1,128)} %bitcast.5, f32[1,4096]{1,0:T(1,128)} %bitcast.6, ...), custom_call_target="tpu_custom_call" | custom-call | tf_op jit(solution)/shard_map/pallas_call | solution.py:1099
  111.7 1.7 %copy.14 = bf16[32,4096]{1,0:T(8,128)(2,1)} copy(bf16[32,4096]{1,0:T(8,128)(2,1)} %shard_map.118) | data formatting | bytes 524288

commit v4 on v3

--- a/solution.py
+++ b/solution.py
@@ -421,6 +421,7 @@
 GPARTS = 4
 HPARTS = 4
 PLANES = 4
+MPARTS = 4
 
 
 def plane_orders(length):
@@ -483,12 +484,12 @@
 
     def pair_copy(h):
         return pltpu.make_async_remote_copy(
-            own16.at[h], peer.at[h], psend.at[0, h], precv.at[0, h], pair, MESH
+            own16.at[h], peer.at[h], psend.at[0], precv.at[0, h], pair, MESH
         )
 
     def line_copy(h):
         return pltpu.make_async_remote_copy(
-            cout.at[h], cin.at[h], psend.at[1, h], precv.at[1, h], me.dev(dp=1), MESH
+            cout.at[h], cin.at[h], psend.at[1], precv.at[1, h], me.dev(dp=1), MESH
         )
 
     tot_copy = pltpu.make_async_remote_copy(tots.at[0], tots.at[1], tsem.at[0], tsem.at[1], pair, MESH)
@@ -541,7 +542,7 @@
     peer_in = jnp.where(is_odd, one, jnp.zeros_like(mine))
 
     peers = (dict(dc=1), dict(dy=1), dict(dy=1, dc=1))
-    pieces = 2
+    pieces = MPARTS
     span = width // pieces
 
     def mix_copy(k, i):
@@ -549,14 +550,14 @@
         cols = pl.ds(i * span, span)
         src = flat.at[pl.ds(pl.multiple_of(to[1] * rows, rows), rows), cols]
         return pltpu.make_async_remote_copy(
-            src, tok.at[e, :, cols], msend.at[k, i], mrecv.at[k, i], to, MESH
+            src, tok.at[e, :, cols], msend.at[0], mrecv.at[k, i], to, MESH
         )
 
     def mix_in(k, i):
         to = me.dev(**peers[k])
         cols = pl.ds(i * span, span)
         return pltpu.make_async_remote_copy(
-            tok.at[to[1], :, cols], tok.at[to[1], :, cols], msend.at[k, i], mrecv.at[k, i], to, MESH
+            tok.at[to[1], :, cols], tok.at[to[1], :, cols], msend.at[0], mrecv.at[k, i], to, MESH
         )
 
     def f_chain(h):
@@ -632,13 +633,13 @@
     x_out[:, n_exp * width :] = extra.astype(bf)
 
     def finish():
+        def out(ref, sent):
+            pltpu.make_async_remote_copy(ref, ref, sent, sent, pair, MESH).wait_send()
+
         tot_copy.wait_send()
-        for h in range(heads):
-            pair_copy(h).wait_send()
-            pl.when(z < L - 1)(lambda: line_copy(h).wait_send())
-        for i in range(pieces):
-            for k in range(len(peers)):
-                mix_copy(k, i).wait_send()
+        out(own16, psend.at[0])
+        pl.when(z < L - 1)(lambda: out(cout, psend.at[1]))
+        out(tok.at[pl.ds(0, len(peers))], msend.at[0])
 
     return finish
 
@@ -648,7 +649,7 @@
     wg_ref, wu_ref, wd_ref, out_ref,
     xs, ys, act, sib, din, xin, yin, lin, tot, wg, wu, wd, hid_ref,
     own16, peer, cin, cout, tots, tok,
-    gsend, grecv, bsend, brecv, ssend, srecv, loc, psend, precv, tsem, msend, mrecv,
+    gsend, lsend, grecv, crecv, brecv, ssend, srecv, loc, psend, precv, tsem, msend, mrecv,
 ):
     me = Place(n_seq, n_exp)
     L, p = me.length, me.p
@@ -682,64 +683,61 @@
     def prow(q):
         return pl.ds(pl.multiple_of(q * rows, rows), rows)
 
-    def gcopy(kind, q, part, r, to, skind=None):
+    def gcopy(kind, q, part, r, to, sent=None):
         ref = xs.at[r, gcols[part]]
-        skind = kind if skind is None else skind
-        return pltpu.make_async_remote_copy(
-            ref, ref, gsend.at[skind, q, part], grecv.at[kind, q, part], to, MESH
-        )
+        sent = gsend.at[kind] if sent is None else sent
+        got = crecv.at[q] if kind == 0 else grecv.at[kind - 1, q, part]
+        return pltpu.make_async_remote_copy(ref, ref, sent, got, to, MESH)
+
+    def bulk(ref, sent):
+        return pltpu.make_async_remote_copy(ref, ref, sent, sent, X, MESH)
 
     upper = GPARTS // 2
-
-    def line_pair(q, part, do):
+    cut = gcols[upper].start
+    low_cols, high_cols = pl.ds(0, cut), pl.ds(cut, xs.shape[1] - cut)
+
+    def line_pair(q, part):
         pl.when(jnp.logical_and(q >= p, p > 0))(
-            lambda: do(gcopy(0, q, part, row(q), me.dev(dp=-1)))
+            lambda: gcopy(5, q, part, row(q), me.dev(dp=-1), lsend.at[0, q]).start()
         )
         pl.when(jnp.logical_and(q <= p, p + 1 < L))(
-            lambda: do(gcopy(0, q, part, row(q), me.dev(dp=1), 9))
-        )
-
-    def start(cp):
-        cp.start()
+            lambda: gcopy(5, q, part, row(q), me.dev(dp=1), lsend.at[1, q]).start()
+        )
 
     def g_line(q, part):
-        pl.when(q != p)(lambda: gcopy(0, q, part, row(q), X).wait_recv())
-        line_pair(q, part, start)
-
-    def first(q, part):
-        return [gcopy(2, q, part, row(q), Y), gcopy(5, q, part, row(q), C)]
+        pl.when(q != p)(lambda: gcopy(5, q, part, row(q), X).wait_recv())
+        line_pair(q, part)
 
     def second_x(q, part):
-        out = [gcopy(6, q, part, row(q, 1, 0), C)]
+        out = [gcopy(0, q, part, row(q, 1, 0), C)]
         return out if part >= upper else [gcopy(3, q, part, row(q, 1, 0), Y)] + out
 
     def second_y(q, part):
-        out = [gcopy(7, q, part, row(q, 0, 1), C)]
+        out = [gcopy(0, q, part, row(q, 0, 1), C)]
         return out if part < upper else [gcopy(4, q, part, row(q, 0, 1), X)] + out
 
     def third(q, part):
-        return [gcopy(8, q, part, row(q, 1, 1), C)]
+        return [gcopy(0, q, part, row(q, 1, 1), C)]
 
     lower, higher = range(upper), range(upper, GPARTS)
 
-    def g_first(q, turn):
+    def g_first(q, turn, own=False):
         for part in lower if turn == 0 else higher:
-            gcopy(1, q, part, row(q), X).start()
+            gcopy(1, q, part, row(q), X, gsend.at[5 + turn] if own else None).start()
         for part in higher if turn == 0 else lower:
             gcopy(2, q, part, row(q), Y).start()
         if turn == 0:
             for part in range(GPARTS):
-                gcopy(5, q, part, row(q), C).start()
+                gcopy(0, q, part, row(q), C).start()
 
     def g_own(q):
         for part in lower:
-            line_pair(q, part, start)
-        g_first(q, 0)
-        for part in lower:
-            gcopy(1, q, part, row(q), X).wait_send()
+            line_pair(q, part)
+        g_first(q, 0, True)
+        bulk(xs.at[row(q), low_cols], gsend.at[5]).wait_send()
         for part in higher:
-            line_pair(q, part, start)
-        g_first(q, 1)
+            line_pair(q, part)
+        g_first(q, 1, True)
 
     def from_x(q, part):
         gcopy(1, q, part, row(q, 1, 0), X).wait_recv()
@@ -773,33 +771,30 @@
             when(jnp.logical_and(q >= 0, q < L), lambda: [g_line(q, part) for part in parts])
 
     def g_done(q):
-        for part in range(GPARTS):
-            gcopy(5, q, part, row(q, 0, 0, 1), X).wait_recv()
-            gcopy(6, q, part, row(q, 1, 0, 1), X).wait_recv()
-            gcopy(7, q, part, row(q, 0, 1, 1), X).wait_recv()
-            gcopy(8, q, part, row(q, 1, 1, 1), X).wait_recv()
-
-    def g_drain(q):
-        for part in range(GPARTS):
-            line_pair(q, part, lambda cp: cp.wait_send())
-            across = gcopy(1, q, part, row(q), X)
-            if part < upper:
-                pl.when(q != p)(lambda: across.wait_send())
-            else:
-                across.wait_send()
-            for cp in first(q, part) + second_x(q, part) + second_y(q, part) + third(q, part):
-                cp.wait_send()
+        r = pl.ds(pl.multiple_of((q * 2 + 1 - me.c) * 4 * rows, 4 * rows), 4 * rows)
+        pltpu.make_async_remote_copy(xs.at[r], xs.at[r], gsend.at[0], crecv.at[q], X, MESH).wait_recv()
+
+    def g_drain():
+        bulk(xs.at[pl.ds(0, L * 4 * rows)], gsend.at[0]).wait_send()
+        bulk(xs.at[pl.ds(0, (L - 1) * rows)], gsend.at[1]).wait_send()
+        bulk(xs.at[pl.ds(0, L * rows)], gsend.at[2]).wait_send()
+        bulk(xs.at[pl.ds(0, L * rows), low_cols], gsend.at[3]).wait_send()
+        bulk(xs.at[pl.ds(0, L * rows), high_cols], gsend.at[4]).wait_send()
+        bulk(xs.at[row(p), high_cols], gsend.at[6]).wait_send()
+        for q in range(L):
+            pl.when(jnp.logical_and(q >= p, p > 0))(lambda: bulk(xs.at[row(q)], lsend.at[0, q]).wait_send())
+            pl.when(jnp.logical_and(q <= p, p + 1 < L))(lambda: bulk(xs.at[row(q)], lsend.at[1, q]).wait_send())
 
     def sib_copy(q, h):
         r = pl.ds(pl.multiple_of((q * 2 + 1 - me.c) * 4 * rows, 4 * rows), 4 * rows)
         d = pl.ds(pl.multiple_of(q * 4 * rows, 4 * rows), 4 * rows)
         return pltpu.make_async_remote_copy(
-            ys.at[r, hcols[h]], sib.at[d, hcols[h]], bsend.at[q, h], brecv.at[q, h], C, MESH
+            ys.at[r, hcols[h]], sib.at[d, hcols[h]], ssend.at[4], brecv.at[q, h], C, MESH
         )
 
     def scopy(kind, q, h, r, dst, d, to):
         return pltpu.make_async_remote_copy(
-            ys.at[r, hcols[h]], dst.at[d, hcols[h]], ssend.at[kind, q, h], srecv.at[kind, q, h], to, MESH
+            ys.at[r, hcols[h]], dst.at[d, hcols[h]], ssend.at[kind], srecv.at[kind, q, h], to, MESH
         )
 
     def diag_copy(q, h):
@@ -818,7 +813,7 @@
         return pltpu.make_async_remote_copy(
             ys.at[row(q), hcols[h]],
             lin.at[prow(slot), hcols[h]],
-            ssend.at[3, q, h],
+            ssend.at[3],
             srecv.at[3, slot, h],
             me.dev(dp=2 * up - 1),
             MESH,
@@ -826,7 +821,7 @@
 
     def line_in(slot, h):
         return pltpu.make_async_remote_copy(
-            ys.at[row(p), hcols[h]], lin.at[prow(slot), hcols[h]], ssend.at[3, p, h], srecv.at[3, slot, h], X, MESH
+            ys.at[row(p), hcols[h]], lin.at[prow(slot), hcols[h]], ssend.at[3], srecv.at[3, slot, h], X, MESH
         )
 
     def pair(q, h, dx, dy):
@@ -892,13 +887,10 @@
     def r_early(q, h):
         pl.when(jnp.logical_and(at_end, q != p))(lambda: r_line(q, h))
 
-    def r_drain(q):
-        for h in range(HPARTS):
-            sib_copy(q, h).wait_send()
-            diag_copy(q, h).wait_send()
-            x_copy(q, h).wait_send()
-            y_copy(q, h).wait_send()
-            pl.when(q != p)(lambda: line_copy(q, h).wait_send())
+    def r_drain():
+        bulk(sib, ssend.at[4]).wait_send()
+        for kind, ref in enumerate((din, xin, yin, lin.at[pl.ds(0, (L - 1) * rows)])):
+            bulk(ref, ssend.at[kind]).wait_send()
 
     tile = next(t for t in range(512, 0, -128) if hidden % t == 0)
     fsteps = hidden // tile
@@ -986,6 +978,7 @@
             if n == 2:
                 ahead(lambda: g_rest(nxt))
                 later(lambda: settle(older, 2), lambda: settle(older, 3))
+                closing(lambda: r_second(prev, 2))
 
         g_done(q)
         for f in range(fsteps):
@@ -996,19 +989,20 @@
         for h in range(HPARTS):
             ffn_out(q, h)
             if h == 0:
-                after(lambda: r_second(prev, 2))
+                ahead(lambda: r_second(prev, 2))
+                closing(lambda: r_second(prev, 3))
             if h == 1:
-                after(lambda: r_second(prev, 3))
+                ahead(lambda: r_second(prev, 3))
                 opening(lambda: g_ring(3, range(GPARTS)), lambda: g_first(third, 0))
+                closing(lambda: settle(prev, 0))
             if h == 2:
                 r_first(q, 0)
                 ahead(lambda: g_third(nxt))
                 opening(lambda: g_third(nxt))
-                closing(lambda: settle(prev, 0))
+                closing(lambda: settle(prev, 1))
             if h == 3:
                 r_first(q, 1)
                 opening(lambda: g_first(third, 1))
-                closing(lambda: settle(prev, 1))
         return carry
 
     def one_line(i, h):
@@ -1035,12 +1029,8 @@
             r_last(h - 1)
     r_last(HPARTS - 1)
 
-    def drain(q, carry):
-        g_drain(q)
-        r_drain(q)
-        return carry
-
-    lax.fori_loop(0, L, drain, 0)
+    g_drain()
+    r_drain()
 
 
 def moe_scratch(n_seq, n_exp, x_shape, w_shape):
@@ -1077,6 +1067,7 @@
         and n_seq * n_exp == 8 * PLANES
         and w_shape[1] % 128 == 0
         and w_shape[2] % (128 * HPARTS) == 0
+        and w_shape[2] // n_exp % (128 * MPARTS) == 0
         and need + 6 * 2**20 <= MOE_VMEM
     )
 
@@ -1110,18 +1101,19 @@
             states,
             pltpu.VMEM((2, heads + -heads % 8, dim), jnp.float32),
             pltpu.VMEM((n_exp, rows, part), bf),
-            dma((10, L, GPARTS)),
-            dma((10, L, GPARTS)),
+            dma((7,)),
+            dma((2, L)),
+            dma((5, L, GPARTS)),
+            dma((L,)),
             dma((L, HPARTS)),
-            dma((L, HPARTS)),
-            dma((4, L + 1, HPARTS)),
+            dma((5,)),
             dma((4, L + 1, HPARTS)),
             dma((3,)),
-            dma((2, heads)),
+            dma((2,)),
             dma((2, heads)),
             dma((2,)),
-            dma((3, 2)),
-            dma((3, 2)),
+            dma((1,)),
+            dma((3, MPARTS)),
         ],
         compiler_params=pltpu.CompilerParams(
             collective_id=5, has_side_effects=True, vmem_limit_bytes=MOE_VMEM

time: 114 us -> 110 us (0.965)
  Pallas kernels: 112 us -> 107 us
    pallas_call x1, Pallas kernels: 112 us -> 107 us  [whole_layer(): pl.pallas_call(functools.partial(moe_kernel, n_seq, n_exp), out_shape=jax...]
where the time goes in v4:
time: 110 us; the launch traced here: 109 us
  Pallas kernels  107 us (97%)
  local copies, waits for them, and re-layouts  1.67 us (2%)
    pallas_call x1, Pallas kernels, whole_layer(): pl.pallas_call(functools.partial(moe_kernel, n_seq, n_exp), out_shape=jax...  107 us

profile of v4, /device:TPU:8, one launch (start us, length us, event | category | flops | bytes accessed | tf_op | source)
XLA Modules:
  0.0 109.1 jit_solution(9274472772663611236)
XLA Ops:
  0.0 107.5 %shard_map.118 = bf16[32,4096]{1,0:T(8,128)(2,1)} custom-call(bf16[128,1024]{1,0:T(8,128)(2,1)} %q_ref.1, bf16[128,1024]{1,0:T(8,128)(2,1)} %k_ref.1, bf16[128,1024]{1,0:T(8,128)(2,1)} %v_ref.1, f32[8,128]{1,0:T(8,128)} %bitcast.7, bf16[32,4096]{1,0:T(8,128)(2,1)} %res_ref.1, f32[1,4096]{1,0:T(1,128)} %bitcast.5, f32[1,4096]{1,0:T(1,128)} %bitcast.6, ...), custom_call_target="tpu_custom_call" | custom-call | tf_op jit(solution)/shard_map/pallas_call | solution.py:1090
  107.5 1.7 %copy.14 = bf16[32,4096]{1,0:T(8,128)(2,1)} copy(bf16[32,4096]{1,0:T(8,128)(2,1)} %shard_map.118) | data formatting | bytes 524288

commit v5 on v4

--- a/solution.py
+++ b/solution.py
@@ -649,7 +649,7 @@
     wg_ref, wu_ref, wd_ref, out_ref,
     xs, ys, act, sib, din, xin, yin, lin, tot, wg, wu, wd, hid_ref,
     own16, peer, cin, cout, tots, tok,
-    gsend, lsend, grecv, crecv, brecv, ssend, srecv, loc, psend, precv, tsem, msend, mrecv,
+    gsend, lsend, grecv, crecv, brecv, ssend, srecv, drecv, loc, psend, precv, tsem, msend, mrecv,
 ):
     me = Place(n_seq, n_exp)
     L, p = me.length, me.p
@@ -660,7 +660,7 @@
     X, Y, C = me.dev(dx=1), me.dev(dy=1), me.dev(dc=1)
     visit, lines = plane_orders(L)
     gcols = spans(xs.shape[1] // 128, GPARTS)
-    hcols = spans(width // 128, HPARTS)
+    hcols, dcols = spans(width // 128, HPARTS), spans(width // 128, 2 * HPARTS)
 
     loads = [
         pltpu.make_async_copy(a.at[0], b, loc.at[i])
@@ -708,16 +708,45 @@
         pl.when(q != p)(lambda: gcopy(5, q, part, row(q), X).wait_recv())
         line_pair(q, part)
 
-    def second_x(q, part):
+    middle = range(1, GPARTS - 1)
+    mid_cols = pl.ds(gcols[1].start, gcols[-1].start - gcols[1].start)
+
+    def second_x(q, part, own):
         out = [gcopy(0, q, part, row(q, 1, 0), C)]
-        return out if part >= upper else [gcopy(3, q, part, row(q, 1, 0), Y)] + out
-
-    def second_y(q, part):
+        if own and part < upper:
+            out.append(gcopy(3, q, part, row(q, 1, 0), Y, gsend.at[7]))
+        if not own and part == 0:
+            out.append(gcopy(3, q, part, row(q, 1, 0), Y))
+        return out
+
+    def second_y(q, part, own):
         out = [gcopy(0, q, part, row(q, 0, 1), C)]
-        return out if part < upper else [gcopy(4, q, part, row(q, 0, 1), X)] + out
-
-    def third(q, part):
-        return [gcopy(0, q, part, row(q, 1, 1), C)]
+        if own and part >= upper:
+            out.append(gcopy(4, q, part, row(q, 0, 1), X, gsend.at[8]))
+        if not own and part == GPARTS - 1:
+            out.append(gcopy(4, q, part, row(q, 0, 1), X))
+        return out
+
+    def corner_out(q):
+        for part in middle:
+            pl.when(jnp.logical_and(q >= p, p > 0))(
+                lambda: gcopy(6, q, part, row(q, 1, 1), me.dev(dp=-1), lsend.at[2, q]).start()
+            )
+            pl.when(jnp.logical_and(q <= p, p + 1 < L))(
+                lambda: gcopy(6, q, part, row(q, 1, 1), me.dev(dp=1), lsend.at[3, q]).start()
+            )
+
+    def g_corner(k):
+        for sign in (-1, 1):
+            q = p + sign * k
+
+            def arrive():
+                for part in middle:
+                    gcopy(6, q, part, row(q, 1, 1), X).wait_recv()
+                    gcopy(0, q, part, row(q, 1, 1), C).start()
+                corner_out(q)
+
+            when(jnp.logical_and(q >= 0, q < L), arrive)
 
     lower, higher = range(upper), range(upper, GPARTS)
 
@@ -739,31 +768,32 @@
             line_pair(q, part)
         g_first(q, 1, True)
 
-    def from_x(q, part):
+    def from_x(q, part, own):
         gcopy(1, q, part, row(q, 1, 0), X).wait_recv()
-        for cp in second_x(q, part):
+        for cp in second_x(q, part, own)[::-1]:
             cp.start()
 
-    def from_y(q, part):
+    def from_y(q, part, own):
         gcopy(2, q, part, row(q, 0, 1), X).wait_recv()
-        for cp in second_y(q, part):
+        for cp in second_y(q, part, own)[::-1]:
             cp.start()
 
-    def g_second(q):
+    def g_second(q, own=False):
         for part in lower:
-            from_x(q, part)
-            from_y(q, part + upper)
-
-    def g_rest(q):
+            from_x(q, part, own)
+            from_y(q, GPARTS - 1 - part, own)
+
+    def g_rest(q, own=False):
         for part in lower:
-            from_x(q, part + upper)
-            from_y(q, part)
-
-    def g_third(q):
-        for part in range(GPARTS):
+            from_x(q, part + upper, own)
+            from_y(q, part, own)
+
+    def g_third(q, own=False):
+        for part in range(GPARTS) if own else (0, GPARTS - 1):
             gcopy(3 if part < upper else 4, q, part, row(q, 1, 1), X).wait_recv()
-            for cp in third(q, part):
-                cp.start()
+            gcopy(0, q, part, row(q, 1, 1), C).start()
+        if own:
+            corner_out(q)
 
     def g_ring(k, parts):
         for sign in (-1, 1):
@@ -778,12 +808,17 @@
         bulk(xs.at[pl.ds(0, L * 4 * rows)], gsend.at[0]).wait_send()
         bulk(xs.at[pl.ds(0, (L - 1) * rows)], gsend.at[1]).wait_send()
         bulk(xs.at[pl.ds(0, L * rows)], gsend.at[2]).wait_send()
-        bulk(xs.at[pl.ds(0, L * rows), low_cols], gsend.at[3]).wait_send()
-        bulk(xs.at[pl.ds(0, L * rows), high_cols], gsend.at[4]).wait_send()
+        bulk(xs.at[pl.ds(0, (L - 1) * rows), gcols[0]], gsend.at[3]).wait_send()
+        bulk(xs.at[pl.ds(0, (L - 1) * rows), gcols[-1]], gsend.at[4]).wait_send()
+        bulk(xs.at[row(p), low_cols], gsend.at[7]).wait_send()
+        bulk(xs.at[row(p), high_cols], gsend.at[8]).wait_send()
         bulk(xs.at[row(p), high_cols], gsend.at[6]).wait_send()
         for q in range(L):
             pl.when(jnp.logical_and(q >= p, p > 0))(lambda: bulk(xs.at[row(q)], lsend.at[0, q]).wait_send())
             pl.when(jnp.logical_and(q <= p, p + 1 < L))(lambda: bulk(xs.at[row(q)], lsend.at[1, q]).wait_send())
+            mid = xs.at[row(q), mid_cols]
+            pl.when(jnp.logical_and(q >= p, p > 0))(lambda: bulk(mid, lsend.at[2, q]).wait_send())
+            pl.when(jnp.logical_and(q <= p, p + 1 < L))(lambda: bulk(mid, lsend.at[3, q]).wait_send())
 
     def sib_copy(q, h):
         r = pl.ds(pl.multiple_of((q * 2 + 1 - me.c) * 4 * rows, 4 * rows), 4 * rows)
@@ -797,8 +832,11 @@
             ys.at[r, hcols[h]], dst.at[d, hcols[h]], ssend.at[kind], srecv.at[kind, q, h], to, MESH
         )
 
-    def diag_copy(q, h):
-        return scopy(0, q, h, row(q, 1, 1), din, prow(q), Y if 2 * h < HPARTS else X)
+    def diag_copy(q, h, side):
+        cols = dcols[2 * h + side]
+        return pltpu.make_async_remote_copy(
+            ys.at[row(q, 1, 1), cols], din.at[prow(q), cols], ssend.at[0], drecv.at[side, q, h], (Y, X)[side], MESH
+        )
 
     def x_copy(q, h):
         return scopy(1, q, h, row(q, 1, 0), xin, prow(q), X)
@@ -830,19 +868,19 @@
     def r_first(q, h):
         sib_copy(q, h).wait_recv()
         ys[row(q, 1, 1), hcols[h]] = pair(q, h, 1, 1).astype(bf)
-        diag_copy(q, h).start()
+        for side in range(2):
+            diag_copy(q, h, side).start()
 
     def r_second(q, h):
         sx, sy = pair(q, h, 1, 0), pair(q, h, 0, 1)
-        diag_copy(q, h).wait_recv()
-        more = din[prow(q), hcols[h]].astype(f32)
-        if 2 * h < HPARTS:
-            sx = sx + more
-        else:
-            sy = sy + more
-        ys[row(q, 1, 0), hcols[h]] = sx.astype(bf)
+        near, far = dcols[2 * h], dcols[2 * h + 1]
+        diag_copy(q, h, 0).wait_recv()
+        ys[row(q, 1, 0), near] = (sx[:, : near.size] + din[prow(q), near].astype(f32)).astype(bf)
+        ys[row(q, 1, 0), far] = sx[:, near.size :].astype(bf)
         x_copy(q, h).start()
-        ys[row(q, 0, 1), hcols[h]] = sy.astype(bf)
+        diag_copy(q, h, 1).wait_recv()
+        ys[row(q, 0, 1), near] = sy[:, : near.size].astype(bf)
+        ys[row(q, 0, 1), far] = (sy[:, near.size :] + din[prow(q), far].astype(f32)).astype(bf)
         y_copy(q, h).start()
 
     def r_third(q, h):
@@ -926,12 +964,12 @@
     )
     second = pick(visit, p, 1)
     g_own(p)
-    g_second(p)
+    g_second(p, True)
     g_ring(1, lower)
-    g_rest(p)
+    g_rest(p, True)
     g_ring(1, higher)
     g_first(second, 0)
-    g_third(p)
+    g_third(p, True)
     g_first(second, 1)
     front_done()
     for cp in loads:
@@ -972,10 +1010,12 @@
                 )
             if n == 1:
                 opening(lambda: g_rest(nxt), lambda: g_first(fourth, 1))
+                when(j == 1, lambda: g_corner(3))
                 ahead(lambda: g_second(nxt))
                 later(lambda: settle(older, 0), lambda: settle(older, 1))
                 after(lambda: r_second(prev, 0), lambda: r_second(prev, 1))
             if n == 2:
+                opening(lambda: g_corner(1))
                 ahead(lambda: g_rest(nxt))
                 later(lambda: settle(older, 2), lambda: settle(older, 3))
                 closing(lambda: r_second(prev, 2))
@@ -1002,7 +1042,7 @@
                 closing(lambda: settle(prev, 1))
             if h == 3:
                 r_first(q, 1)
-                opening(lambda: g_first(third, 1))
+                opening(lambda: g_first(third, 1), lambda: g_corner(2))
         return carry
 
     def one_line(i, h):
@@ -1066,7 +1106,7 @@
         and n_exp // 4 == 1
         and n_seq * n_exp == 8 * PLANES
         and w_shape[1] % 128 == 0
-        and w_shape[2] % (128 * HPARTS) == 0
+        and w_shape[2] % (256 * HPARTS) == 0
         and w_shape[2] // n_exp % (128 * MPARTS) == 0
         and need + 6 * 2**20 <= MOE_VMEM
     )
@@ -1101,13 +1141,14 @@
             states,
             pltpu.VMEM((2, heads + -heads % 8, dim), jnp.float32),
             pltpu.VMEM((n_exp, rows, part), bf),
-            dma((7,)),
-            dma((2, L)),
-            dma((5, L, GPARTS)),
+            dma((9,)),
+            dma((4, L)),
+            dma((6, L, GPARTS)),
             dma((L,)),
             dma((L, HPARTS)),
             dma((5,)),
             dma((4, L + 1, HPARTS)),
+            dma((2, L, HPARTS)),
             dma((3,)),
             dma((2,)),
             dma((2, heads)),

time: 110 us -> 107 us (0.973)
  Pallas kernels: 107 us -> 105 us
    pallas_call x1, Pallas kernels: 107 us -> 105 us  [whole_layer(): pl.pallas_call(functools.partial(moe_kernel, n_seq, n_exp), out_shape=jax...]
where the time goes in v5:
time: 107 us
  Pallas kernels  105 us (98%)
  local copies, waits for them, and re-layouts  1.67 us (2%)
    pallas_call x1, Pallas kernels, whole_layer(): pl.pallas_call(functools.partial(moe_kernel, n_seq, n_exp), out_shape=jax...  105 us

profile of v5, /device:TPU:8, one launch (start us, length us, event | category | flops | bytes accessed | tf_op | source)
XLA Modules:
  0.0 106.8 jit_solution(9444640227449529336)
XLA Ops:
  0.0 105.1 %shard_map.118 = bf16[32,4096]{1,0:T(8,128)(2,1)} custom-call(bf16[128,1024]{1,0:T(8,128)(2,1)} %q_ref.1, bf16[128,1024]{1,0:T(8,128)(2,1)} %k_ref.1, bf16[128,1024]{1,0:T(8,128)(2,1)} %v_ref.1, f32[8,128]{1,0:T(8,128)} %bitcast.7, bf16[32,4096]{1,0:T(8,128)(2,1)} %res_ref.1, f32[1,4096]{1,0:T(1,128)} %bitcast.5, f32[1,4096]{1,0:T(1,128)} %bitcast.6, ...), custom_call_target="tpu_custom_call" | custom-call | tf_op jit(solution)/shard_map/pallas_call | solution.py:1130
  105.1 1.7 %copy.14 = bf16[32,4096]{1,0:T(8,128)(2,1)} copy(bf16[32,4096]{1,0:T(8,128)(2,1)} %shard_map.118) | data formatting | bytes 524288

commit v6 on v5

--- a/solution.py
+++ b/solution.py
@@ -550,14 +550,13 @@
         cols = pl.ds(i * span, span)
         src = flat.at[pl.ds(pl.multiple_of(to[1] * rows, rows), rows), cols]
         return pltpu.make_async_remote_copy(
-            src, tok.at[e, :, cols], msend.at[0], mrecv.at[k, i], to, MESH
-        )
-
-    def mix_in(k, i):
+            src, tok.at[e, :, cols], msend.at[0], mrecv.at[k], to, MESH
+        )
+
+    def mix_in(k):
         to = me.dev(**peers[k])
-        cols = pl.ds(i * span, span)
-        return pltpu.make_async_remote_copy(
-            tok.at[to[1], :, cols], tok.at[to[1], :, cols], msend.at[0], mrecv.at[k, i], to, MESH
+        return pltpu.make_async_remote_copy(
+            tok.at[to[1]], tok.at[to[1]], msend.at[0], mrecv.at[k], to, MESH
         )
 
     def f_chain(h):
@@ -598,9 +597,8 @@
     tok[e] = flat[pl.ds(pl.multiple_of(e * rows, rows), rows), 0:width]
 
     def f_mix():
-        for i in range(pieces):
-            for k in range(len(peers)):
-                mix_in(k, i).wait_recv()
+        for k in range(len(peers)):
+            mix_in(k).wait_recv()
 
     f_mix()
     square = jnp.zeros((rows, 1), f32)
@@ -647,9 +645,9 @@
 def moe_kernel(
     n_seq, n_exp, q_ref, k_ref, v_ref, ld_ref, res_ref, ag_ref, mg_ref, ids_ref, gw_ref,
     wg_ref, wu_ref, wd_ref, out_ref,
-    xs, ys, act, sib, din, xin, yin, lin, tot, wg, wu, wd, hid_ref,
+    xs, ys, act, sib, din, near_in, lin, tot, wg, wu, wd, hid_ref,
     own16, peer, cin, cout, tots, tok,
-    gsend, lsend, grecv, crecv, brecv, ssend, srecv, drecv, loc, psend, precv, tsem, msend, mrecv,
+    gsend, lsend, grecv, drecv, crecv, brecv, ssend, srecv, nrecv, drecv2, loc, psend, precv, tsem, msend, mrecv,
 ):
     me = Place(n_seq, n_exp)
     L, p = me.length, me.p
@@ -683,122 +681,105 @@
     def prow(q):
         return pl.ds(pl.multiple_of(q * rows, rows), rows)
 
-    def gcopy(kind, q, part, r, to, sent=None):
-        ref = xs.at[r, gcols[part]]
-        sent = gsend.at[kind] if sent is None else sent
-        got = crecv.at[q] if kind == 0 else grecv.at[kind - 1, q, part]
+    cut = gcols[GPARTS // 2].start
+    halves = (pl.ds(0, cut), pl.ds(cut, xs.shape[1] - cut))
+    middle = pl.ds(gcols[1].start, gcols[-1].start - gcols[1].start)
+    lower, higher, both = (0,), (1,), (0, 1)
+
+    def gcopy(q, cols, r, to, sent, got):
+        ref = xs.at[r, cols]
         return pltpu.make_async_remote_copy(ref, ref, sent, got, to, MESH)
+
+    def arrive(q, cols, r, got):
+        gcopy(q, cols, r, X, gsend.at[0], got).wait_recv()
 
     def bulk(ref, sent):
         return pltpu.make_async_remote_copy(ref, ref, sent, sent, X, MESH)
 
-    upper = GPARTS // 2
-    cut = gcols[upper].start
-    low_cols, high_cols = pl.ds(0, cut), pl.ds(cut, xs.shape[1] - cut)
-
-    def line_pair(q, part):
+    def to_sibling(q, cols, r):
+        gcopy(q, cols, r, C, gsend.at[0], crecv.at[q]).start()
+
+    def both_ways(q, cols, r, lane, got):
         pl.when(jnp.logical_and(q >= p, p > 0))(
-            lambda: gcopy(5, q, part, row(q), me.dev(dp=-1), lsend.at[0, q]).start()
+            lambda: gcopy(q, cols, r, me.dev(dp=-1), lsend.at[lane, q], got).start()
         )
         pl.when(jnp.logical_and(q <= p, p + 1 < L))(
-            lambda: gcopy(5, q, part, row(q), me.dev(dp=1), lsend.at[1, q]).start()
-        )
-
-    def g_line(q, part):
-        pl.when(q != p)(lambda: gcopy(5, q, part, row(q), X).wait_recv())
-        line_pair(q, part)
-
-    middle = range(1, GPARTS - 1)
-    mid_cols = pl.ds(gcols[1].start, gcols[-1].start - gcols[1].start)
-
-    def second_x(q, part, own):
-        out = [gcopy(0, q, part, row(q, 1, 0), C)]
-        if own and part < upper:
-            out.append(gcopy(3, q, part, row(q, 1, 0), Y, gsend.at[7]))
-        if not own and part == 0:
-            out.append(gcopy(3, q, part, row(q, 1, 0), Y))
-        return out
-
-    def second_y(q, part, own):
-        out = [gcopy(0, q, part, row(q, 0, 1), C)]
-        if own and part >= upper:
-            out.append(gcopy(4, q, part, row(q, 0, 1), X, gsend.at[8]))
-        if not own and part == GPARTS - 1:
-            out.append(gcopy(4, q, part, row(q, 0, 1), X))
-        return out
+            lambda: gcopy(q, cols, r, me.dev(dp=1), lsend.at[lane + 1, q], got).start()
+        )
+
+    def line_pair(q, side):
+        both_ways(q, halves[side], row(q), 0, grecv.at[2, q, side])
 
     def corner_out(q):
-        for part in middle:
-            pl.when(jnp.logical_and(q >= p, p > 0))(
-                lambda: gcopy(6, q, part, row(q, 1, 1), me.dev(dp=-1), lsend.at[2, q]).start()
-            )
-            pl.when(jnp.logical_and(q <= p, p + 1 < L))(
-                lambda: gcopy(6, q, part, row(q, 1, 1), me.dev(dp=1), lsend.at[3, q]).start()
-            )
+        both_ways(q, middle, row(q, 1, 1), 2, drecv.at[q, 2])
+
+    def g_first(q, turn, own=False):
+        sent = gsend.at[5 + turn] if own else gsend.at[1]
+        gcopy(q, halves[turn], row(q), X, sent, grecv.at[0, q, turn]).start()
+        gcopy(q, halves[1 - turn], row(q), Y, gsend.at[2], grecv.at[1, q, 1 - turn]).start()
+        if turn == 0:
+            to_sibling(q, pl.ds(0, xs.shape[1]), row(q))
+
+    def g_own(q):
+        line_pair(q, 0)
+        g_first(q, 0, True)
+        bulk(xs.at[row(q), halves[0]], gsend.at[5]).wait_send()
+        line_pair(q, 1)
+        g_first(q, 1, True)
+
+    def from_x(q, side, own):
+        r = row(q, 1, 0)
+        arrive(q, halves[side], r, grecv.at[0, q, side])
+        if side == 0:
+            cols, sent = (halves[0], gsend.at[7]) if own else (gcols[0], gsend.at[3])
+            gcopy(q, cols, r, Y, sent, drecv.at[q, 0]).start()
+        to_sibling(q, halves[side], r)
+
+    def from_y(q, side, own):
+        r = row(q, 0, 1)
+        arrive(q, halves[side], r, grecv.at[1, q, side])
+        if side == 1:
+            cols, sent = (halves[1], gsend.at[8]) if own else (gcols[-1], gsend.at[4])
+            gcopy(q, cols, r, X, sent, drecv.at[q, 1]).start()
+        to_sibling(q, halves[side], r)
+
+    def g_second(q, own=False):
+        from_x(q, 0, own)
+        from_y(q, 1, own)
+
+    def g_rest(q, own=False):
+        from_x(q, 1, own)
+        from_y(q, 0, own)
+
+    def g_third(q, own=False):
+        r = row(q, 1, 1)
+        for k, cols in enumerate(halves if own else (gcols[0], gcols[-1])):
+            arrive(q, cols, r, drecv.at[q, k])
+            to_sibling(q, cols, r)
+        if own:
+            corner_out(q)
 
     def g_corner(k):
         for sign in (-1, 1):
             q = p + sign * k
 
-            def arrive():
-                for part in middle:
-                    gcopy(6, q, part, row(q, 1, 1), X).wait_recv()
-                    gcopy(0, q, part, row(q, 1, 1), C).start()
+            def pass_on():
+                arrive(q, middle, row(q, 1, 1), drecv.at[q, 2])
                 corner_out(q)
-
-            when(jnp.logical_and(q >= 0, q < L), arrive)
-
-    lower, higher = range(upper), range(upper, GPARTS)
-
-    def g_first(q, turn, own=False):
-        for part in lower if turn == 0 else higher:
-            gcopy(1, q, part, row(q), X, gsend.at[5 + turn] if own else None).start()
-        for part in higher if turn == 0 else lower:
-            gcopy(2, q, part, row(q), Y).start()
-        if turn == 0:
-            for part in range(GPARTS):
-                gcopy(0, q, part, row(q), C).start()
-
-    def g_own(q):
-        for part in lower:
-            line_pair(q, part)
-        g_first(q, 0, True)
-        bulk(xs.at[row(q), low_cols], gsend.at[5]).wait_send()
-        for part in higher:
-            line_pair(q, part)
-        g_first(q, 1, True)
-
-    def from_x(q, part, own):
-        gcopy(1, q, part, row(q, 1, 0), X).wait_recv()
-        for cp in second_x(q, part, own)[::-1]:
-            cp.start()
-
-    def from_y(q, part, own):
-        gcopy(2, q, part, row(q, 0, 1), X).wait_recv()
-        for cp in second_y(q, part, own)[::-1]:
-            cp.start()
-
-    def g_second(q, own=False):
-        for part in lower:
-            from_x(q, part, own)
-            from_y(q, GPARTS - 1 - part, own)
-
-    def g_rest(q, own=False):
-        for part in lower:
-            from_x(q, part + upper, own)
-            from_y(q, part, own)
-
-    def g_third(q, own=False):
-        for part in range(GPARTS) if own else (0, GPARTS - 1):
-            gcopy(3 if part < upper else 4, q, part, row(q, 1, 1), X).wait_recv()
-            gcopy(0, q, part, row(q, 1, 1), C).start()
-        if own:
-            corner_out(q)
-
-    def g_ring(k, parts):
+                to_sibling(q, middle, row(q, 1, 1))
+
+            when(jnp.logical_and(q >= 0, q < L), pass_on)
+
+    def g_ring(k, sides):
         for sign in (-1, 1):
             q = p + sign * k
-            when(jnp.logical_and(q >= 0, q < L), lambda: [g_line(q, part) for part in parts])
+
+            def pass_on():
+                for side in sides:
+                    arrive(q, halves[side], row(q), grecv.at[2, q, side])
+                    line_pair(q, side)
+
+            when(jnp.logical_and(q >= 0, q < L), pass_on)
 
     def g_done(q):
         r = pl.ds(pl.multiple_of((q * 2 + 1 - me.c) * 4 * rows, 4 * rows), 4 * rows)
@@ -810,13 +791,13 @@
         bulk(xs.at[pl.ds(0, L * rows)], gsend.at[2]).wait_send()
         bulk(xs.at[pl.ds(0, (L - 1) * rows), gcols[0]], gsend.at[3]).wait_send()
         bulk(xs.at[pl.ds(0, (L - 1) * rows), gcols[-1]], gsend.at[4]).wait_send()
-        bulk(xs.at[row(p), low_cols], gsend.at[7]).wait_send()
-        bulk(xs.at[row(p), high_cols], gsend.at[8]).wait_send()
-        bulk(xs.at[row(p), high_cols], gsend.at[6]).wait_send()
+        bulk(xs.at[row(p), halves[0]], gsend.at[7]).wait_send()
+        bulk(xs.at[row(p), halves[1]], gsend.at[8]).wait_send()
+        bulk(xs.at[row(p), halves[1]], gsend.at[6]).wait_send()
         for q in range(L):
             pl.when(jnp.logical_and(q >= p, p > 0))(lambda: bulk(xs.at[row(q)], lsend.at[0, q]).wait_send())
             pl.when(jnp.logical_and(q <= p, p + 1 < L))(lambda: bulk(xs.at[row(q)], lsend.at[1, q]).wait_send())
-            mid = xs.at[row(q), mid_cols]
+            mid = xs.at[row(q), middle]
             pl.when(jnp.logical_and(q >= p, p > 0))(lambda: bulk(mid, lsend.at[2, q]).wait_send())
             pl.when(jnp.logical_and(q <= p, p + 1 < L))(lambda: bulk(mid, lsend.at[3, q]).wait_send())
 
@@ -827,22 +808,25 @@
             ys.at[r, hcols[h]], sib.at[d, hcols[h]], ssend.at[4], brecv.at[q, h], C, MESH
         )
 
-    def scopy(kind, q, h, r, dst, d, to):
-        return pltpu.make_async_remote_copy(
-            ys.at[r, hcols[h]], dst.at[d, hcols[h]], ssend.at[kind], srecv.at[kind, q, h], to, MESH
-        )
+    def plane_copy(side, q, h, r, to):
+        return pltpu.make_async_remote_copy(
+            ys.at[r, hcols[h]], near_in.at[prow(2 * q + side), hcols[h]], ssend.at[1 + side], nrecv.at[q, h], to, MESH
+        )
+
+    def settled(ref, got):
+        pltpu.make_async_remote_copy(ref, ref, ssend.at[0], got, X, MESH).wait_recv()
 
     def diag_copy(q, h, side):
         cols = dcols[2 * h + side]
         return pltpu.make_async_remote_copy(
-            ys.at[row(q, 1, 1), cols], din.at[prow(q), cols], ssend.at[0], drecv.at[side, q, h], (Y, X)[side], MESH
+            ys.at[row(q, 1, 1), cols], din.at[prow(q), cols], ssend.at[0], drecv2.at[q, h], (Y, X)[side], MESH
         )
 
     def x_copy(q, h):
-        return scopy(1, q, h, row(q, 1, 0), xin, prow(q), X)
+        return plane_copy(0, q, h, row(q, 1, 0), X)
 
     def y_copy(q, h):
-        return scopy(2, q, h, row(q, 0, 1), yin, prow(q), Y)
+        return plane_copy(1, q, h, row(q, 0, 1), Y)
 
     def line_copy(q, h):
         up = (q > p).astype(jnp.int32)
@@ -852,14 +836,14 @@
             ys.at[row(q), hcols[h]],
             lin.at[prow(slot), hcols[h]],
             ssend.at[3],
-            srecv.at[3, slot, h],
+            srecv.at[slot, h],
             me.dev(dp=2 * up - 1),
             MESH,
         )
 
     def line_in(slot, h):
         return pltpu.make_async_remote_copy(
-            ys.at[row(p), hcols[h]], lin.at[prow(slot), hcols[h]], ssend.at[3], srecv.at[3, slot, h], X, MESH
+            ys.at[row(p), hcols[h]], lin.at[prow(slot), hcols[h]], ssend.at[3], srecv.at[slot, h], X, MESH
         )
 
     def pair(q, h, dx, dy):
@@ -874,20 +858,19 @@
     def r_second(q, h):
         sx, sy = pair(q, h, 1, 0), pair(q, h, 0, 1)
         near, far = dcols[2 * h], dcols[2 * h + 1]
-        diag_copy(q, h, 0).wait_recv()
+        settled(din.at[prow(q), hcols[h]], drecv2.at[q, h])
         ys[row(q, 1, 0), near] = (sx[:, : near.size] + din[prow(q), near].astype(f32)).astype(bf)
         ys[row(q, 1, 0), far] = sx[:, near.size :].astype(bf)
         x_copy(q, h).start()
-        diag_copy(q, h, 1).wait_recv()
         ys[row(q, 0, 1), near] = sy[:, : near.size].astype(bf)
         ys[row(q, 0, 1), far] = (sy[:, near.size :] + din[prow(q), far].astype(f32)).astype(bf)
         y_copy(q, h).start()
 
     def r_third(q, h):
         total = pair(q, h, 0, 0)
-        x_copy(q, h).wait_recv()
-        y_copy(q, h).wait_recv()
-        total = total + xin[prow(q), hcols[h]].astype(f32) + yin[prow(q), hcols[h]].astype(f32)
+        settled(near_in.at[pl.ds(pl.multiple_of(2 * q * rows, rows), 2 * rows), hcols[h]], nrecv.at[q, h])
+        for side in range(2):
+            total = total + near_in[prow(2 * q + side), hcols[h]].astype(f32)
         tot[prow(q), hcols[h]] = total
 
     def r_line(q, h):
@@ -927,8 +910,8 @@
 
     def r_drain():
         bulk(sib, ssend.at[4]).wait_send()
-        for kind, ref in enumerate((din, xin, yin, lin.at[pl.ds(0, (L - 1) * rows)])):
-            bulk(ref, ssend.at[kind]).wait_send()
+        for kind in range(3):
+            bulk(din, ssend.at[kind]).wait_send()
 
     tile = next(t for t in range(512, 0, -128) if hidden % t == 0)
     fsteps = hidden // tile
@@ -1033,7 +1016,7 @@
                 closing(lambda: r_second(prev, 3))
             if h == 1:
                 ahead(lambda: r_second(prev, 3))
-                opening(lambda: g_ring(3, range(GPARTS)), lambda: g_first(third, 0))
+                opening(lambda: g_ring(3, both), lambda: g_first(third, 0))
                 closing(lambda: settle(prev, 0))
             if h == 2:
                 r_first(q, 0)
@@ -1051,26 +1034,28 @@
     lax.fori_loop(0, L, chunk, 0)
 
     final, prior = pick(visit, p, L - 1), pick(visit, p, L - 2)
-    r_first(final, 2)
-    r_first(final, 3)
     for h in (2, 3):
         r_third(prior, h)
         r_early(prior, h)
+    for h in (2, 3):
+        r_first(final, h)
     for h in range(HPARTS):
         r_second(final, h)
-        one_line(0, h)
+        if h:
+            one_line(0, h - 1)
+    one_line(0, HPARTS - 1)
     for h in range(HPARTS):
         one_line(1, h)
         r_third(final, h)
         r_early(final, h)
+    g_drain()
     for h in range(HPARTS):
         one_line(2, h)
         if h:
             r_last(h - 1)
+    r_drain()
     r_last(HPARTS - 1)
-
-    g_drain()
-    r_drain()
+    bulk(lin.at[pl.ds(0, (L - 1) * rows)], ssend.at[3]).wait_send()
 
 
 def moe_scratch(n_seq, n_exp, x_shape, w_shape):
@@ -1084,8 +1069,7 @@
         ((8 * rows, hidden), bf),
         ((n // 2 * rows, width), bf),
         ((L * rows, width), bf),
-        ((L * rows, width), bf),
-        ((L * rows, width), bf),
+        ((2 * L * rows, width), bf),
         ((L * rows + rows, width), bf),
         ((L * rows, width), f32),
         ((hidden, width), bf),
@@ -1143,18 +1127,20 @@
             pltpu.VMEM((n_exp, rows, part), bf),
             dma((9,)),
             dma((4, L)),
-            dma((6, L, GPARTS)),
+            dma((3, L, 2)),
+            dma((L, 3)),
             dma((L,)),
             dma((L, HPARTS)),
             dma((5,)),
-            dma((4, L + 1, HPARTS)),
-            dma((2, L, HPARTS)),
+            dma((L + 1, HPARTS)),
+            dma((L, HPARTS)),
+            dma((L, HPARTS)),
             dma((3,)),
             dma((2,)),
             dma((2, heads)),
             dma((2,)),
             dma((1,)),
-            dma((3, MPARTS)),
+            dma((3,)),
         ],
         compiler_params=pltpu.CompilerParams(
             collective_id=5, has_side_effects=True, vmem_limit_bytes=MOE_VMEM

time: 107 us -> 106 us (level)
  no operation moved by 1% of the time
where the time goes in v6:
time: 106 us
  Pallas kernels  104 us (98%)
  local copies, waits for them, and re-layouts  1.67 us (2%)
    pallas_call x1, Pallas kernels, whole_layer(): pl.pallas_call(functools.partial(moe_kernel, n_seq, n_exp), out_shape=jax...  104 us

profile of v6, /device:TPU:8, one launch (start us, length us, event | category | flops | bytes accessed | tf_op | source)
XLA Modules:
  0.0 105.8 jit_solution(915698843730348229)
XLA Ops:
  0.0 104.1 %shard_map.118 = bf16[32,4096]{1,0:T(8,128)(2,1)} custom-call(bf16[128,1024]{1,0:T(8,128)(2,1)} %q_ref.1, bf16[128,1024]{1,0:T(8,128)(2,1)} %k_ref.1, bf16[128,1024]{1,0:T(8,128)(2,1)} %v_ref.1, f32[8,128]{1,0:T(8,128)} %bitcast.7, bf16[32,4096]{1,0:T(8,128)(2,1)} %res_ref.1, f32[1,4096]{1,0:T(1,128)} %bitcast.5, f32[1,4096]{1,0:T(1,128)} %bitcast.6, ...), custom_call_target="tpu_custom_call" | custom-call | tf_op jit(solution)/shard_map/pallas_call | solution.py:1114
  104.1 1.7 %copy.14 = bf16[32,4096]{1,0:T(8,128)(2,1)} copy(bf16[32,4096]{1,0:T(8,128)(2,1)} %shard_map.118) | data formatting | bytes 524288

commit v7 on v6

--- a/solution.py
+++ b/solution.py
@@ -723,7 +723,6 @@
     def g_own(q):
         line_pair(q, 0)
         g_first(q, 0, True)
-        bulk(xs.at[row(q), halves[0]], gsend.at[5]).wait_send()
         line_pair(q, 1)
         g_first(q, 1, True)
 
@@ -793,6 +792,7 @@
         bulk(xs.at[pl.ds(0, (L - 1) * rows), gcols[-1]], gsend.at[4]).wait_send()
         bulk(xs.at[row(p), halves[0]], gsend.at[7]).wait_send()
         bulk(xs.at[row(p), halves[1]], gsend.at[8]).wait_send()
+        bulk(xs.at[row(p), halves[0]], gsend.at[5]).wait_send()
         bulk(xs.at[row(p), halves[1]], gsend.at[6]).wait_send()
         for q in range(L):
             pl.when(jnp.logical_and(q >= p, p > 0))(lambda: bulk(xs.at[row(q)], lsend.at[0, q]).wait_send())
@@ -985,6 +985,7 @@
         def hook(n):
             if n == 0:
                 after(lambda: r_first(prev, 2), lambda: r_first(prev, 3))
+                when(j == 1, lambda: g_corner(2))
                 opening(
                     lambda: g_ring(2, lower),
                     lambda: g_second(nxt),
@@ -993,7 +994,6 @@
                 )
             if n == 1:
                 opening(lambda: g_rest(nxt), lambda: g_first(fourth, 1))
-                when(j == 1, lambda: g_corner(3))
                 ahead(lambda: g_second(nxt))
                 later(lambda: settle(older, 0), lambda: settle(older, 1))
                 after(lambda: r_second(prev, 0), lambda: r_second(prev, 1))
@@ -1015,6 +1015,7 @@
                 ahead(lambda: r_second(prev, 2))
                 closing(lambda: r_second(prev, 3))
             if h == 1:
+                when(j == 1, lambda: g_corner(3))
                 ahead(lambda: r_second(prev, 3))
                 opening(lambda: g_ring(3, both), lambda: g_first(third, 0))
                 closing(lambda: settle(prev, 0))
@@ -1025,7 +1026,7 @@
                 closing(lambda: settle(prev, 1))
             if h == 3:
                 r_first(q, 1)
-                opening(lambda: g_first(third, 1), lambda: g_corner(2))
+                opening(lambda: g_first(third, 1))
         return carry
 
     def one_line(i, h):
@@ -1034,11 +1035,12 @@
     lax.fori_loop(0, L, chunk, 0)
 
     final, prior = pick(visit, p, L - 1), pick(visit, p, L - 2)
-    for h in (2, 3):
-        r_third(prior, h)
-        r_early(prior, h)
-    for h in (2, 3):
-        r_first(final, h)
+    r_first(final, 2)
+    r_third(prior, 2)
+    r_early(prior, 2)
+    r_first(final, 3)
+    r_third(prior, 3)
+    r_early(prior, 3)
     for h in range(HPARTS):
         r_second(final, h)
         if h:

time: 106 us -> 105 us (level)
  no operation moved by 1% of the time
where the time goes in v7:
time: 105 us
  Pallas kernels  103 us (98%)
  local copies, waits for them, and re-layouts  1.67 us (2%)
    pallas_call x1, Pallas kernels, whole_layer(): pl.pallas_call(functools.partial(moe_kernel, n_seq, n_exp), out_shape=jax...  103 us

profile of v7, /device:TPU:8, one launch (start us, length us, event | category | flops | bytes accessed | tf_op | source)
XLA Modules:
  0.0 104.9 jit_solution(17943505271722903969)
XLA Ops:
  0.0 103.2 %shard_map.118 = bf16[32,4096]{1,0:T(8,128)(2,1)} custom-call(bf16[128,1024]{1,0:T(8,128)(2,1)} %q_ref.1, bf16[128,1024]{1,0:T(8,128)(2,1)} %k_ref.1, bf16[128,1024]{1,0:T(8,128)(2,1)} %v_ref.1, f32[8,128]{1,0:T(8,128)} %bitcast.7, bf16[32,4096]{1,0:T(8,128)(2,1)} %res_ref.1, f32[1,4096]{1,0:T(1,128)} %bitcast.5, f32[1,4096]{1,0:T(1,128)} %bitcast.6, ...), custom_call_target="tpu_custom_call" | custom-call | tf_op jit(solution)/shard_map/pallas_call | solution.py:1116
  103.3 1.7 %copy.14 = bf16[32,4096]{1,0:T(8,128)(2,1)} copy(bf16[32,4096]{1,0:T(8,128)(2,1)} %shard_map.118) | data formatting | bytes 524288

commit v8 on v7

--- a/solution.py
+++ b/solution.py
@@ -647,7 +647,7 @@
     wg_ref, wu_ref, wd_ref, out_ref,
     xs, ys, act, sib, din, near_in, lin, tot, wg, wu, wd, hid_ref,
     own16, peer, cin, cout, tots, tok,
-    gsend, lsend, grecv, drecv, crecv, brecv, ssend, srecv, nrecv, drecv2, loc, psend, precv, tsem, msend, mrecv,
+    gsend, lsend, grecv, drecv, crecv, brecv, ssend, srecv, drecv2, loc, psend, precv, tsem, msend, mrecv,
 ):
     me = Place(n_seq, n_exp)
     L, p = me.length, me.p
@@ -810,7 +810,7 @@
 
     def plane_copy(side, q, h, r, to):
         return pltpu.make_async_remote_copy(
-            ys.at[r, hcols[h]], near_in.at[prow(2 * q + side), hcols[h]], ssend.at[1 + side], nrecv.at[q, h], to, MESH
+            ys.at[r, hcols[h]], near_in.at[prow(2 * q + side), hcols[h]], ssend.at[1 + side], brecv.at[q, h], to, MESH
         )
 
     def settled(ref, got):
@@ -868,7 +868,7 @@
 
     def r_third(q, h):
         total = pair(q, h, 0, 0)
-        settled(near_in.at[pl.ds(pl.multiple_of(2 * q * rows, rows), 2 * rows), hcols[h]], nrecv.at[q, h])
+        settled(near_in.at[pl.ds(pl.multiple_of(2 * q * rows, rows), 2 * rows), hcols[h]], brecv.at[q, h])
         for side in range(2):
             total = total + near_in[prow(2 * q + side), hcols[h]].astype(f32)
         tot[prow(q), hcols[h]] = total
@@ -1135,7 +1135,6 @@
             dma((L, HPARTS)),
             dma((5,)),
             dma((L + 1, HPARTS)),
-            dma((L, HPARTS)),
             dma((L, HPARTS)),
             dma((3,)),
             dma((2,)),

time: 105 us -> 105 us (level)
  no operation moved by 1% of the time
where the time goes in v8:
time: 105 us
  Pallas kernels  103 us (98%)
  local copies, waits for them, and re-layouts  1.67 us (2%)
    pallas_call x1, Pallas kernels, whole_layer(): pl.pallas_call(functools.partial(moe_kernel, n_seq, n_exp), out_shape=jax...  103 us

profile of v8, /device:TPU:8, one launch (start us, length us, event | category | flops | bytes accessed | tf_op | source)
XLA Modules:
  0.0 104.8 jit_solution(15620403235948838394)
XLA Ops:
  0.0 103.1 %shard_map.118 = bf16[32,4096]{1,0:T(8,128)(2,1)} custom-call(bf16[128,1024]{1,0:T(8,128)(2,1)} %q_ref.1, bf16[128,1024]{1,0:T(8,128)(2,1)} %k_ref.1, bf16[128,1024]{1,0:T(8,128)(2,1)} %v_ref.1, f32[8,128]{1,0:T(8,128)} %bitcast.7, bf16[32,4096]{1,0:T(8,128)(2,1)} %res_ref.1, f32[1,4096]{1,0:T(1,128)} %bitcast.5, f32[1,4096]{1,0:T(1,128)} %bitcast.6, ...), custom_call_target="tpu_custom_call" | custom-call | tf_op jit(solution)/shard_map/pallas_call | solution.py:1116
  103.1 1.7 %copy.14 = bf16[32,4096]{1,0:T(8,128)(2,1)} copy(bf16[32,4096]{1,0:T(8,128)(2,1)} %shard_map.118) | data formatting | bytes 524288
